TPU v7x, 32 devices: a whole 2x2x4 slice. The times are simulated.
32 devices in a mesh: shard: 4 (over z), ctx: 2 (over core), tp: 4 (over y, x).
Axes of the slice: x: 2, y: 2, z: 4, core: 2. Of those that a mesh axis runs over, the one named last changes fastest.
Arguments:
- tokens: bfloat16 [16384, 896], P(('shard', 'ctx', 'tp')), may hold values from -6 to 6
- doc_ids: int32 [16, 1024], P(('shard', 'tp')), may hold values from -1 to 7, as said below
- w_query: bfloat16 [896, 896], P(('shard', 'ctx')), may hold values from -0.1875 to 0.1875
- b_query: bfloat16 [896], P(('shard', 'ctx')), may hold values from -3 to 3
- key_projection: bfloat16 [896, 128], P(('shard', 'ctx')), may hold values from -0.1875 to 0.1875
- key_bias_vector: bfloat16 [128], P(('shard', 'ctx')), may hold values from -3 to 3
- value_projection: bfloat16 [896, 128], P(('shard', 'ctx')), may hold values from -0.1875 to 0.1875
- value_bias_vector: bfloat16 [128], P(('shard', 'ctx')), may hold values from -3 to 3
- w_output: bfloat16 [896, 896], P(('shard', 'ctx')), may hold values from -1.5 to 1.5
- gain_attn: bfloat16 [896], P(('shard', 'ctx')), may hold values from 0.5 to 1.5
- gain_mlp: bfloat16 [896], P(('shard', 'ctx')), may hold values from 0.5 to 1.5
- w_gate: bfloat16 [896, 4864], P(('shard', 'ctx'), 'tp'), may hold values from -0.1875 to 0.1875
- w_up: bfloat16 [896, 4864], P(('shard', 'ctx'), 'tp'), may hold values from -0.1875 to 0.1875
- w_down: bfloat16 [4864, 896], P('tp', ('shard', 'ctx')), may hold values from -0.078125 to 0.078125
- cotangent: bfloat16 [16384, 896], P(('shard', 'ctx', 'tp')), may hold values from -6 to 6
Outputs:
- output: bfloat16 [16384, 896], P(('shard', 'ctx', 'tp'))
- grad_tokens: bfloat16 [16384, 896], P(('shard', 'ctx', 'tp'))
- grad_w_query: float32 [896, 896], P(('shard', 'ctx'))
- grad_b_query: float32 [896], P(('shard', 'ctx'))
- grad_w_key: float32 [896, 128], P(('shard', 'ctx'))
- grad_b_key: float32 [128], P(('shard', 'ctx'))
- grad_w_value: float32 [896, 128], P(('shard', 'ctx'))
- grad_b_value: float32 [128], P(('shard', 'ctx'))
- grad_w_output: float32 [896, 896], P(('shard', 'ctx'))
- grad_gain_attn: float32 [896], P(('shard', 'ctx'))
- grad_gain_mlp: float32 [896], P(('shard', 'ctx'))
- grad_w_gate: float32 [896, 4864], P(('shard', 'ctx'), 'tp')
- grad_w_up: float32 [896, 4864], P(('shard', 'ctx'), 'tp')
- grad_w_down: float32 [4864, 896], P('tp', ('shard', 'ctx'))
Inputs may be any that keep to these rules, and one draw needn't show every extreme that they name: `doc_ids`: documents begin at multiples of 128 within a buffer, are numbered 0, 1, 2 in order in each buffer, and only the rest of a document's last block of 128 slots is padding (-1).
All inputs are finite; a program needn't handle non-finite values.
Results may differ from a plain program's by a relative error of at most 0.02.
Values may be sent and summed in bfloat16 or wider, within the bound.
No kernel may reach another device: no remote copies, remote signals or barrier semaphores. Data moves between devices by JAX's collectives and lax.ppermute only.
A program may use at most 192 MiB of HBM per device.

v0:
```python
import functools

import jax
import jax.numpy as jnp
from jax import lax
from jax.experimental import pallas as pl
from jax.experimental.pallas import tpu as pltpu
from jax.sharding import PartitionSpec as P


QUERY_HEADS = 14
KEY_VALUE_HEADS = 2
HEAD_WIDTH = 64
GROUP = QUERY_HEADS // KEY_VALUE_HEADS
HEADS_PER_STEP = 1

EPSILON = 1e-06
THETA = 1000000.0
NEGATIVE = -1e30
BF = jnp.bfloat16
F32 = jnp.float32


def dot(left, right, left_dim, right_dim, out=F32):
    return lax.dot_general(
        left, right, (((left_dim,), (right_dim,)), ((), ())), preferred_element_type=out
    )


def fill_bias(bias, doc_row, doc_col, row_start, row_count, span):
    keys = lax.broadcasted_iota(jnp.int32, (span, row_count), 0)
    queries = lax.broadcasted_iota(jnp.int32, (span, row_count), 1) + row_start
    key_doc = doc_col[0:span, :]
    query_doc = doc_row[:, row_start : row_start + row_count]
    same = (key_doc == query_doc) & (query_doc >= 0) & (keys <= queries)
    bias[0:span, :] = jnp.where(same | (keys == queries), 0.0, NEGATIVE)


def load_keys(half, own, other, keys_t, keys, values_t, values):
    width = KEY_VALUE_HEADS * HEAD_WIDTH
    parts = (own,) if half == 0 else (other, own)
    for place, part in enumerate(parts):
        count = part.shape[1]
        rows = slice(place * count, (place + 1) * count)
        key_t = part[0:width, :]
        value_t = part[width : 2 * width, :]
        keys_t[:, rows] = key_t
        values_t[:, rows] = value_t
        key = key_t.astype(F32).T.astype(BF)
        for head in range(KEY_VALUE_HEADS):
            lanes = slice(head * HEAD_WIDTH, (head + 1) * HEAD_WIDTH)
            keys[head, rows, :] = key[:, lanes]
        if values is not None:
            value = value_t.astype(F32).T.astype(BF)
            for head in range(KEY_VALUE_HEADS):
                lanes = slice(head * HEAD_WIDTH, (head + 1) * HEAD_WIDTH)
                values[head, rows, :] = value[:, lanes]


def attention_forward_body(
    half_ref, doc_row, doc_col, query_t, own, other, mixed_t, lse, keys_t, keys, values_t, bias
):
    token_count = query_t.shape[1]
    step = token_count // 2
    for half in (0, 1):

        @pl.when(half_ref[0] == half)
        def _():
            load_keys(half, own, other, keys_t, keys, values_t, None)
            for block in (0, 1):
                span = half * token_count + (block + 1) * step
                start = half * token_count + block * step
                cols = slice(block * step, (block + 1) * step)
                fill_bias(bias, doc_row, doc_col, start, step, span)

                def one(head):
                    group = lax.div(head, GROUP)
                    head_rows = pl.ds(pl.multiple_of(group * HEAD_WIDTH, HEAD_WIDTH), HEAD_WIDTH)
                    place = pl.ds(pl.multiple_of(head * HEAD_WIDTH, HEAD_WIDTH), HEAD_WIDTH)
                    score = (
                        jnp.dot(
                            keys[group, 0:span, :],
                            query_t[place, cols],
                            preferred_element_type=F32,
                        )
                        + bias[0:span, :]
                    )
                    top = jnp.max(score, axis=0, keepdims=True)
                    weight = jnp.exp(score - top)
                    total = jnp.sum(weight, axis=0, keepdims=True)
                    out = jnp.dot(
                        values_t[head_rows, 0:span],
                        weight.astype(BF),
                        preferred_element_type=F32,
                    )
                    mixed_t[place, cols] = (out / total).astype(BF)
                    lse[head, :, cols] = jnp.broadcast_to(top + jnp.log(total), (8, step))

                def several(index, carry):
                    for extra in range(HEADS_PER_STEP):
                        one(index * HEADS_PER_STEP + extra)
                    return carry

                lax.fori_loop(0, QUERY_HEADS // HEADS_PER_STEP, several, 0)


def attention_forward(half, doc_row, doc_col, query_t, own, other):
    width, token_count = query_t.shape
    kv = KEY_VALUE_HEADS * HEAD_WIDTH
    vmem = pl.BlockSpec(memory_space=pltpu.VMEM)
    return pl.pallas_call(
        attention_forward_body,
        out_shape=(
            jax.ShapeDtypeStruct((width, token_count), BF),
            jax.ShapeDtypeStruct((QUERY_HEADS, 8, token_count), F32),
        ),
        in_specs=[pl.BlockSpec(memory_space=pltpu.SMEM)] + [vmem] * 5,
        out_specs=(vmem, vmem),
        scratch_shapes=[
            pltpu.VMEM((kv, 2 * token_count), BF),
            pltpu.VMEM((KEY_VALUE_HEADS, 2 * token_count, HEAD_WIDTH), BF),
            pltpu.VMEM((kv, 2 * token_count), BF),
            pltpu.VMEM((2 * token_count, token_count // 2), F32),
        ],
        cost_estimate=pl.CostEstimate(
            flops=int(15e9), bytes_accessed=4 * width * token_count, transcendentals=0
        ),
        name="attention_forward",
    )(half, doc_row, doc_col, query_t, own, other)


def attention_backward_body(
    half_ref,
    doc_row,
    doc_col,
    query_t,
    own,
    other,
    grad_t,
    lse,
    grad_query_t,
    own_sums,
    other_sums,
    grad_key,
    grad_value,
    keys_t,
    keys,
    values_t,
    values,
    bias,
):
    token_count = query_t.shape[1]
    step = token_count // 2
    grad_key[...] = jnp.zeros_like(grad_key)
    grad_value[...] = jnp.zeros_like(grad_value)
    for half in (0, 1):

        @pl.when(half_ref[0] == half)
        def _():
            load_keys(half, own, other, keys_t, keys, values_t, values)
            for block in (0, 1):
                span = half * token_count + (block + 1) * step
                start = half * token_count + block * step
                cols = slice(block * step, (block + 1) * step)
                fill_bias(bias, doc_row, doc_col, start, step, span)

                def one(head):
                    group = lax.div(head, GROUP)
                    head_rows = pl.ds(pl.multiple_of(group * HEAD_WIDTH, HEAD_WIDTH), HEAD_WIDTH)
                    place = pl.ds(pl.multiple_of(head * HEAD_WIDTH, HEAD_WIDTH), HEAD_WIDTH)
                    query = query_t[place, cols]
                    grad = grad_t[place, cols]
                    score = (
                        jnp.dot(keys[group, 0:span, :], query, preferred_element_type=F32)
                        + bias[0:span, :]
                    )
                    prob = jnp.exp(score - lse[head, 0:1, cols])
                    grad_prob = jnp.dot(values[group, 0:span, :], grad, preferred_element_type=F32)
                    delta = jnp.sum(prob * grad_prob, axis=0, keepdims=True)
                    grad_score = (prob * (grad_prob - delta)).astype(BF)
                    grad_value[group, 0:span, :] += dot(prob.astype(BF), grad, 1, 1)
                    grad_key[group, 0:span, :] += dot(grad_score, query, 1, 1)
                    grad_query_t[place, cols] = (
                        jnp.dot(keys_t[head_rows, 0:span], grad_score, preferred_element_type=F32)
                        * (HEAD_WIDTH ** (-0.5))
                    ).astype(BF)

                def several(index, carry):
                    for extra in range(HEADS_PER_STEP):
                        one(index * HEADS_PER_STEP + extra)
                    return carry

                lax.fori_loop(0, QUERY_HEADS // HEADS_PER_STEP, several, 0)

            for head in range(2 * KEY_VALUE_HEADS):
                source = (grad_key, grad_value)[head // KEY_VALUE_HEADS]
                rows = slice(head * HEAD_WIDTH, (head + 1) * HEAD_WIDTH)
                first = source[head % KEY_VALUE_HEADS, 0:token_count, :].T
                if half == 0:
                    own_sums[rows, :] = first
                    other_sums[rows, :] = jnp.zeros_like(first)
                else:
                    own_sums[rows, :] = source[head % KEY_VALUE_HEADS, token_count:, :].T
                    other_sums[rows, :] = first


def attention_backward(half, doc_row, doc_col, query_t, own, other, grad_t, lse):
    width, token_count = query_t.shape
    kv = KEY_VALUE_HEADS * HEAD_WIDTH
    vmem = pl.BlockSpec(memory_space=pltpu.VMEM)
    sums = jax.ShapeDtypeStruct((2 * kv, token_count), F32)
    totals = pltpu.VMEM((KEY_VALUE_HEADS, 2 * token_count, HEAD_WIDTH), F32)
    return pl.pallas_call(
        attention_backward_body,
        out_shape=(jax.ShapeDtypeStruct((width, token_count), BF), sums, sums),
        in_specs=[pl.BlockSpec(memory_space=pltpu.SMEM)] + [vmem] * 7,
        out_specs=(vmem, vmem, vmem),
        scratch_shapes=[
            totals,
            totals,
            pltpu.VMEM((kv, 2 * token_count), BF),
            pltpu.VMEM((KEY_VALUE_HEADS, 2 * token_count, HEAD_WIDTH), BF),
            pltpu.VMEM((kv, 2 * token_count), BF),
            pltpu.VMEM((KEY_VALUE_HEADS, 2 * token_count, HEAD_WIDTH), BF),
            pltpu.VMEM((2 * token_count, token_count // 2), F32),
        ],
        cost_estimate=pl.CostEstimate(
            flops=int(35e9), bytes_accessed=8 * width * token_count, transcendentals=0
        ),
        name="attention_backward",
    )(half, doc_row, doc_col, query_t, own, other, grad_t, lse)


def rope_tables(half, token_count):
    half_dim = HEAD_WIDTH // 2
    frequency = THETA ** (-(jnp.arange(half_dim, dtype=F32) * 2.0) / HEAD_WIDTH)
    positions = half * token_count + jnp.arange(token_count, dtype=jnp.int32)
    angles = frequency[:, None] * positions.astype(F32)[None, :]
    return jnp.cos(angles), jnp.sin(angles)


def rotate(values_t, cosine, sine):
    rows, count = values_t.shape
    split = values_t.reshape(rows // HEAD_WIDTH, 2, HEAD_WIDTH // 2, count)
    first, second = split[:, 0], split[:, 1]
    return jnp.stack(
        [first * cosine - second * sine, second * cosine + first * sine], 1
    ).reshape(rows, count)


class Mesh:
    def __init__(self):
        self.shards = lax.axis_size("shard")
        self.ctxs = lax.axis_size("ctx")
        self.tps = lax.axis_size("tp")
        self.fast = (self.shards, self.ctxs, self.tps) == (4, 2, 4)
        self.z = lax.axis_index("shard")
        self.c = lax.axis_index("ctx")
        self.t = lax.axis_index("tp")

    def across(self, value):
        pairs = [(i, self.ctxs - 1 - i) for i in range(self.ctxs)]
        return lax.ppermute(value, "ctx", pairs)

    def side(self, value, which):
        return lax.ppermute(value, "tp", [(i, i ^ which) for i in range(self.tps)])

    def ring(self, value, which):
        return lax.ppermute(value, "shard", [(i, i ^ which) for i in range(self.shards)])

    def place(self):
        return jnp.stack([self.z, self.c, self.t]).astype(jnp.int32)

    def gather_rows(self, block):
        return lax.all_gather(block, ("shard", "ctx"), axis=0)

    def gather_spread(self, block):
        rows, _ = block.shape
        part = rows // self.tps
        quarter = lax.dynamic_slice_in_dim(block, self.t * part, part, 0)
        pieces = [block]
        pieces += [self.ring(quarter, which) for which in (1, 2, 3)]
        far = jnp.concatenate(pieces[1:], 0)
        sides = [self.side(far, which) for which in (1, 2, 3)]
        mine = [block, far] + sides
        theirs = [self.across(piece) for piece in mine]
        return far, sides, mine, theirs

    def gather_line(self, block, later):
        two = self.ring(block, 2)
        one = self.ring(block, 1)
        late, relayed, later = lax.optimization_barrier((block, two, later))
        middle = lax.ppermute(late, "shard", [(1, 2), (2, 1)])
        ends = lax.ppermute(relayed, "shard", [(2, 3), (1, 0)])
        three = jnp.where((self.z == 1) | (self.z == 2), middle, ends)
        return [block, one, two, three]

    def reduce_rows(self, send, keep):
        mine, *quarters = fold(self.place(), keep, self.across(send))
        for which, quarter in enumerate(quarters, 1):
            mine = mine + self.side(quarter, which).astype(F32)
        total = lax.dynamic_index_in_dim(mine, self.z, 0, False)
        for which in (3, 2, 1):
            piece = lax.dynamic_index_in_dim(mine, self.z ^ which, 0, False).astype(BF)
            total = total + self.ring(piece, which).astype(F32)
        low = total.astype(BF)
        one, two, three = (self.side(low, which) for which in (1, 2, 3))
        odd = (self.t & 1) == 1
        a, b = jnp.where(odd, one, low), jnp.where(odd, low, one)
        c, d = jnp.where(odd, three, two), jnp.where(odd, two, three)
        far = self.t >= 2
        return jnp.concatenate(
            [
                jnp.where(far, c, a),
                jnp.where(far, d, b),
                jnp.where(far, a, c),
                jnp.where(far, b, d),
            ],
            0,
        ).astype(F32)

    def gather_tokens(self, rows):
        if not self.fast:
            every = lax.all_gather(rows, "tp", axis=0)
            return [
                lax.dynamic_index_in_dim(every, (self.t + i) % self.tps, 0, False)
                for i in range(self.tps)
            ]
        one = self.side(rows, 1)
        two = self.side(rows, 2)
        late, one, two = lax.optimization_barrier((rows, one, two))
        return [rows, one, two, self.side(late, 3)]

    def scatter_tokens(self, parts):
        if not self.fast:
            every = jnp.stack(parts)
            ordered = jnp.stack(
                [
                    lax.dynamic_index_in_dim(every, (i - self.t) % self.tps, 0, False)
                    for i in range(self.tps)
                ]
            )
            return lax.psum_scatter(ordered, "tp", scatter_dimension=0, tiled=False)
        return sum(piece.astype(F32) for piece in self.exchange_tokens(parts))

    def exchange_tokens(self, parts):
        return parts[:1] + [self.side(parts[which], which) for which in (1, 2, 3)]

    def scatter_line(self, send, keep):
        pieces = fold_line(self.place(), keep, self.across(send))
        total = pieces[0]
        for which in (2, 3, 1):
            total = total + self.ring(pieces[which], which).astype(F32)
        return total


def root_inverse(x):
    return lax.rsqrt(jnp.mean(x * x, -1, keepdims=True) + EPSILON)


def project_body(place, *refs):
    mine, theirs = refs[0:5], refs[5:10]
    tokens, cosine, sine, weight, out_weight, query_t, own, gain_one, gain_two = refs[10:19]
    small, fused = refs[19:]
    width, fused_width = weight.shape
    rows = width // 8
    part = mine[0].shape[0] // 4
    z, c, t = place[0], place[1], place[2]
    for block in range(8):
        shard, core = block // 2, block % 2
        for side in range(4):
            first = side * part
            count = min(part, rows - first)

            def put(pieces, index, start):
                value = pieces[index][pl.ds(start, part), :]
                place_rows = slice(block * rows + first, block * rows + first + count)
                weight[place_rows, :] = value[:count, :fused_width]
                out_weight[place_rows, :] = value[:count, fused_width:]
                if count < part:
                    small[block, :, :] = value[count:, 0:128]

            start = pl.multiple_of(jnp.maximum((shard ^ z) - 1, 0) * part, 16)
            for pieces, owned in ((mine, core == c), (theirs, core != c)):

                @pl.when(owned & (shard == z))
                def _():
                    put(pieces, 0, first)

                for which in range(4):

                    @pl.when(owned & (shard != z) & ((side ^ t) == which))
                    def _():
                        put(pieces, 1 + which, start)

    long = jnp.zeros((16, 1024), F32)
    short = jnp.zeros((16, 128), F32)
    for block in range(8):
        piece = small[block].astype(F32)
        wide = jnp.concatenate([piece, jnp.zeros((16, 896), F32)], 1)
        long = long + (pltpu.roll(wide, rows * block, 1) if block else wide)
        short = short + (pltpu.roll(piece, 16 * block, 1) if block else piece)
    bias = jnp.concatenate([long[0:1, :width], short[1:2], short[2:3]], 1)
    gain = long[3:4, :width]
    gain_one[...] = gain
    gain_two[...] = long[4:5, :width]
    x = tokens[...].astype(F32)
    normed = (x * root_inverse(x) * gain).astype(BF)
    fused[...] = (jnp.dot(normed, weight[...], preferred_element_type=F32) + bias).T
    half_dim = HEAD_WIDTH // 2
    query_width = QUERY_HEADS * HEAD_WIDTH
    kv = KEY_VALUE_HEADS * HEAD_WIDTH
    for head in range(QUERY_HEADS + KEY_VALUE_HEADS):
        start = head * HEAD_WIDTH
        one = fused[start : start + half_dim, :]
        two = fused[start + half_dim : start + HEAD_WIDTH, :]
        low = (one * cosine[...] - two * sine[...]).astype(BF)
        high = (two * cosine[...] + one * sine[...]).astype(BF)
        if head < QUERY_HEADS:
            scale = HEAD_WIDTH ** (-0.5)
            query_t[start : start + half_dim, :] = low * BF(scale)
            query_t[start + half_dim : start + HEAD_WIDTH, :] = high * BF(scale)
        else:
            start -= query_width
            own[start : start + half_dim, :] = low
            own[start + half_dim : start + HEAD_WIDTH, :] = high
    own[kv:, :] = fused[query_width + kv :, :].astype(BF)


def project(place, mine, theirs, tokens, cosine, sine, fused_width):
    token_count, width = tokens.shape
    vmem = pl.BlockSpec(memory_space=pltpu.VMEM)
    kv = KEY_VALUE_HEADS * HEAD_WIDTH
    row = jax.ShapeDtypeStruct((1, width), F32)
    return pl.pallas_call(
        project_body,
        out_shape=(
            jax.ShapeDtypeStruct((width, fused_width), BF),
            jax.ShapeDtypeStruct((width, width), BF),
            jax.ShapeDtypeStruct((QUERY_HEADS * HEAD_WIDTH, token_count), BF),
            jax.ShapeDtypeStruct((2 * kv, token_count), BF),
            row,
            row,
        ),
        in_specs=[pl.BlockSpec(memory_space=pltpu.SMEM)] + [vmem] * 13,
        out_specs=(vmem,) * 6,
        scratch_shapes=[
            pltpu.VMEM((8, 16, 128), BF),
            pltpu.VMEM((fused_width, token_count), F32),
        ],
        cost_estimate=pl.CostEstimate(
            flops=int(3e9), bytes_accessed=int(12e6), transcendentals=0
        ),
        name="project",
    )(place, *mine, *theirs, tokens, cosine, sine)


def output_body(tokens, mixed_t, weight, gain, hidden, normed):
    value = tokens[...].astype(F32) + jnp.dot(
        mixed_t[...].T, weight[...], preferred_element_type=F32
    )
    hidden[...] = value
    normed[...] = (value * root_inverse(value) * gain[...]).astype(BF)


def output_projection(tokens, mixed_t, weight, gain):
    vmem = pl.BlockSpec(memory_space=pltpu.VMEM)
    return pl.pallas_call(
        output_body,
        out_shape=(
            jax.ShapeDtypeStruct(tokens.shape, F32),
            jax.ShapeDtypeStruct(tokens.shape, BF),
        ),
        in_specs=[vmem] * 4,
        out_specs=(vmem, vmem),
        cost_estimate=pl.CostEstimate(
            flops=int(1e9), bytes_accessed=int(6e6), transcendentals=0
        ),
        name="output_projection",
    )(tokens, mixed_t, weight, gain)


def middle_body(
    own, one, two, three, hidden, cotangent, weight, gain, grad_hidden, grad_mixed_t, grad_gain
):
    total = own[...].astype(F32) + one[...].astype(F32)
    total = total + two[...].astype(F32) + three[...].astype(F32)
    h = hidden[...]
    inv = root_inverse(h)
    scaled = total * gain[...]
    mean = jnp.mean(scaled * h, -1, keepdims=True)
    value = cotangent[...].astype(F32) + inv * scaled - h * (inv * inv * inv) * mean
    grad_hidden[...] = value
    grad_gain[...] = jnp.sum(total * h * inv, 0, keepdims=True)
    grad_mixed_t[...] = dot(weight[...], value.astype(BF), 1, 1).astype(BF)


def middle(parts, hidden, cotangent, weight, gain):
    vmem = pl.BlockSpec(memory_space=pltpu.VMEM)
    return pl.pallas_call(
        middle_body,
        out_shape=(
            jax.ShapeDtypeStruct(hidden.shape, F32),
            jax.ShapeDtypeStruct(hidden.shape[::-1], BF),
            jax.ShapeDtypeStruct(gain.shape, F32),
        ),
        in_specs=[vmem] * 8,
        out_specs=(vmem, vmem, vmem),
        cost_estimate=pl.CostEstimate(
            flops=int(1e9), bytes_accessed=int(9e6), transcendentals=0
        ),
        name="middle",
    )(*parts, hidden, cotangent, weight, gain)


def fold_body(place, keep, received, mine, *sends):
    part = mine.shape[1]
    for which, out in enumerate((mine,) + sends):
        rows = pl.ds(pl.multiple_of((place[2] ^ which) * part, 16), part)
        value = keep[0, rows, :].astype(F32) + received[0, rows, :].astype(F32)
        out[0] = value.astype(out.dtype)


def fold(place, keep, received):
    blocks, rows, cols = keep.shape
    part = rows // 4
    shape = (blocks, part, cols)
    return pl.pallas_call(
        fold_body,
        grid=(blocks,),
        out_shape=(jax.ShapeDtypeStruct(shape, F32),) + (jax.ShapeDtypeStruct(shape, BF),) * 3,
        in_specs=[pl.BlockSpec(memory_space=pltpu.SMEM)]
        + [pl.BlockSpec((1, rows, cols), lambda i: (i, 0, 0))] * 2,
        out_specs=(pl.BlockSpec((1, part, cols), lambda i: (i, 0, 0)),) * 4,
        cost_estimate=pl.CostEstimate(
            flops=0, bytes_accessed=6 * blocks * rows * cols, transcendentals=0
        ),
        name="fold",
    )(place, keep, received)


def fold_line_body(place, keep, received, *outs):
    for which, out in enumerate(outs):

        @pl.when(pl.program_id(0) == which)
        def _():
            value = keep[0].astype(F32) + received[0].astype(F32)
            out[...] = value.astype(out.dtype)


def fold_line(place, keep, received):
    shape = keep.shape[1:]
    block = pl.BlockSpec((1,) + shape, lambda i, place: (i ^ place[0], 0, 0, 0))
    out = pl.BlockSpec(shape, lambda i, place: (0, 0, 0))
    return pl.pallas_call(
        fold_line_body,
        out_shape=(jax.ShapeDtypeStruct(shape, F32),) + (jax.ShapeDtypeStruct(shape, BF),) * 3,
        grid_spec=pltpu.PrefetchScalarGridSpec(
            num_scalar_prefetch=1, grid=(4,), in_specs=[block] * 2, out_specs=(out,) * 4
        ),
        cost_estimate=pl.CostEstimate(
            flops=0, bytes_accessed=6 * keep.size, transcendentals=0
        ),
        name="fold_line",
    )(place, keep, received)


def assemble_line_body(place, *refs):
    mine, theirs, out = refs[0:4], refs[4:8], refs[8]
    rows = mine[0].shape[0]
    z, c = place[0], place[1]
    for here in range(4):

        @pl.when(z == here)
        def _():
            for block in range(8):
                shard, core = block // 2, block % 2
                left, right = mine[shard ^ here], theirs[shard ^ here]
                out[0, block * rows : (block + 1) * rows, :] = jnp.where(
                    core == c, left[...], right[...]
                )


def assemble_line(place, mine, theirs, count):
    rows, cols = mine[0].shape
    rows = rows // count
    part = pl.BlockSpec((rows, cols), lambda i: (i, 0))
    return pl.pallas_call(
        assemble_line_body,
        grid=(count,),
        out_shape=jax.ShapeDtypeStruct((count, 8 * rows, cols), BF),
        in_specs=[pl.BlockSpec(memory_space=pltpu.SMEM)] + [part] * 8,
        out_specs=pl.BlockSpec((1, 8 * rows, cols), lambda i: (i, 0, 0)),
        cost_estimate=pl.CostEstimate(
            flops=0, bytes_accessed=32 * rows * cols * count, transcendentals=0
        ),
        name="assemble_line",
    )(place, *mine, *theirs)


def projection_gradients_body(
    place,
    grad_query,
    own_sums,
    other_sums,
    cosine,
    sine,
    tokens,
    gain,
    second_gain,
    grad_hidden,
    mixed_t,
    weight,
    grad_tokens,
    send,
    keep,
    fused,
):
    half_dim = HEAD_WIDTH // 2
    query_width, kv = grad_query.shape[0], own_sums.shape[0] // 2
    rows = keep.shape[1] - 16

    def unrotate(value, start):
        first, second = value[:half_dim], value[half_dim:]
        fused[start : start + half_dim, :] = first * cosine[...] + second * sine[...]
        fused[start + half_dim : start + HEAD_WIDTH, :] = (
            second * cosine[...] - first * sine[...]
        )

    for head in range(QUERY_HEADS):
        start = head * HEAD_WIDTH
        unrotate(grad_query[start : start + HEAD_WIDTH, :].astype(F32), start)
    sums = (own_sums[...] + other_sums[...]).astype(BF).astype(F32)
    for head in range(KEY_VALUE_HEADS):
        start = head * HEAD_WIDTH
        unrotate(sums[start : start + HEAD_WIDTH], query_width + start)
    fused[query_width + kv :, :] = sums[kv:]

    exact = fused[...]
    low = exact.astype(BF)
    rest = (exact - low.astype(F32)).astype(BF)
    ones = jnp.ones((16, exact.shape[1]), BF)
    bias = dot(ones, low, 1, 1) + dot(ones, rest, 1, 1)
    low_rows = low.T
    x = tokens[...].astype(F32)
    inv = root_inverse(x)
    normed_t = (x * inv * gain[...]).astype(BF).T
    grad_normed = dot(low_rows, weight[...], 1, 1)
    scaled = grad_normed * gain[...]
    mean = jnp.mean(scaled * x, -1, keepdims=True)
    hidden = grad_hidden[...]
    grad_tokens[...] = (hidden + inv * scaled - x * (inv * inv * inv) * mean).astype(BF)
    grad_gain = jnp.sum(grad_normed * x * inv, 0, keepdims=True)
    left = jnp.dot(normed_t, low_rows, preferred_element_type=F32).astype(BF)
    right = jnp.dot(
        mixed_t[...], hidden.astype(BF), preferred_element_type=F32
    ).astype(BF)
    split = left.shape[1]
    first_row = jnp.concatenate(
        [bias[:8], jnp.broadcast_to(grad_gain, (8, grad_gain.shape[1]))], 1
    )
    second_row = jnp.concatenate(
        [
            jnp.broadcast_to(second_gain[...], (8, second_gain.shape[1])),
            jnp.zeros((8, split), F32),
        ],
        1,
    )
    index = lax.broadcasted_iota(jnp.int32, first_row.shape, 0)
    small = jnp.where(index == 0, first_row, jnp.where(index == 1, second_row, 0.0))
    small = jnp.concatenate([small, jnp.zeros_like(small)], 0).astype(BF)
    for block in range(8):
        shard, core = block // 2, block % 2
        part = slice(block * rows, (block + 1) * rows)
        for out, owned in ((keep, place[1] == core), (send, place[1] != core)):

            @pl.when(owned)
            def _():
                out[shard, 0:rows, 0:split] = left[part]
                out[shard, 0:rows, split:] = right[part]
                out[shard, rows:, :] = small


def projection_gradients(place, *arrays):
    tokens, weight = arrays[5], arrays[10]
    token_count, width = tokens.shape
    fused_width = weight.shape[1]
    half = jax.ShapeDtypeStruct((4, width // 8 + 16, fused_width + width), BF)
    whole = [
        pl.BlockSpec(array.shape, lambda i, n=array.ndim: (0,) * n) for array in arrays
    ]
    return pl.pallas_call(
        projection_gradients_body,
        grid=(1,),
        out_shape=(jax.ShapeDtypeStruct(tokens.shape, BF), half, half),
        in_specs=[pl.BlockSpec(memory_space=pltpu.SMEM)]
        + whole,
        out_specs=(
            pl.BlockSpec(tokens.shape, lambda i: (0, 0)),
            pl.BlockSpec(half.shape, lambda i: (0, 0, 0)),
            pl.BlockSpec(half.shape, lambda i: (0, 0, 0)),
        ),
        scratch_shapes=[pltpu.VMEM((fused_width, token_count), F32)],
        cost_estimate=pl.CostEstimate(
            flops=int(6e9), bytes_accessed=int(16e6), transcendentals=0
        ),
        name="projection_gradients",
    )(place, *arrays)


def mlp_body(chunks, *refs):
    xs, gs = refs[:chunks], refs[chunks : 2 * chunks]
    gate_ref, up_ref, down_ref = refs[2 * chunks : 2 * chunks + 3]
    backs, downs = refs[-2 - 2 * chunks : -2 - chunks], refs[-2 - chunks : -2]
    units, rows_t = refs[-2:]
    x, g = xs[0][...], gs[0][...]
    first = True
    if chunks == 2:
        first = pl.program_id(0) < pl.num_programs(0) // 2
        x, g = jnp.where(first, x, xs[1][...]), jnp.where(first, g, gs[1][...])
    gate = jnp.dot(x, gate_ref[...], preferred_element_type=F32)
    up = jnp.dot(x, up_ref[...], preferred_element_type=F32)
    sig = 1.0 / (1.0 + jnp.exp(-gate))
    silu = gate * sig
    act = (silu * up).astype(BF)
    grad_act = jnp.dot(g, down_ref[...], preferred_element_type=F32)
    grad_gate = (grad_act * up * sig * (1.0 + gate * (1.0 - sig))).astype(BF)
    grad_up = (grad_act * silu).astype(BF)
    back = (dot(grad_gate, gate_ref[...], 1, 1) + dot(grad_up, up_ref[...], 1, 1)).astype(BF)
    down = dot(act, down_ref[...], 1, 1).astype(BF)
    if chunks == 1:
        backs[0][...] = back
        downs[0][...] = down
    else:
        for index, chosen in enumerate((first, jnp.logical_not(first))):

            @pl.when(chosen)
            def _():
                backs[index][...] = back
                downs[index][...] = down

    units[0] = grad_gate
    units[1] = grad_up
    units[2] = act
    rows_t[0] = x.T
    rows_t[1] = g.T


def mlp(xs, gs, weights, kept, first, total):
    chunks = len(xs)
    count, width = xs[0].shape
    units = weights.shape[2]
    step = min(256, count)
    steps = count // step
    offset = first // step
    rows = [
        pl.BlockSpec((step, width), lambda i, n=n: (jnp.clip(i - n * steps, 0, steps - 1), 0))
        for n in range(chunks)
    ]
    whole = [
        pl.BlockSpec(
            (pl.Squeezed(), width, units), lambda i, n=n: (n, 0, 0), pipeline_mode=pl.Buffered(1)
        )
        for n in range(3)
    ]
    partial = jax.ShapeDtypeStruct((count, width), BF)
    kept = list(kept)
    outs = pl.pallas_call(
        functools.partial(mlp_body, chunks),
        grid=(chunks * steps,),
        out_shape=[partial] * (2 * chunks)
        + [
            jax.ShapeDtypeStruct((3, total, units), BF),
            jax.ShapeDtypeStruct((2, width, total), BF),
        ],
        in_specs=rows + rows + whole + [pl.BlockSpec(memory_space=pl.ANY)] * len(kept),
        out_specs=rows
        + rows
        + [
            pl.BlockSpec((3, step, units), lambda i: (0, i + offset, 0)),
            pl.BlockSpec((2, width, step), lambda i: (0, 0, i + offset)),
        ],
        input_output_aliases={2 * chunks + 3 + i: 2 * chunks + i for i in range(len(kept))},
        cost_estimate=pl.CostEstimate(
            flops=12 * chunks * count * width * units,
            bytes_accessed=6 * width * units + 8 * chunks * count * (width + units),
            transcendentals=chunks * count * units,
        ),
        name="mlp",
    )(*xs, *gs, weights, weights, weights, *kept)
    return list(outs[:chunks]), list(outs[chunks : 2 * chunks]), outs[2 * chunks :]


def weight_gradients_body(place, left, right, send, keep, total):
    index, last = pl.program_id(1), pl.num_programs(1) - 1
    rows = send.shape[2]
    value = jnp.dot(left[0], right[0], preferred_element_type=F32)

    @pl.when(index == 0)
    def _():
        total[...] = value

    @pl.when(index > 0)
    def _():
        total[...] += value

    @pl.when(index == last)
    def _():
        for block in range(8):
            shard, core = block // 2, block % 2
            piece = total[block * rows : (block + 1) * rows, :].astype(BF)

            @pl.when(place[1] == core)
            def _():
                keep[shard, 0] = piece

            @pl.when(place[1] != core)
            def _():
                send[shard, 0] = piece


def weight_gradients(place, units, rows_t):
    _, total, wide = units.shape
    width = rows_t.shape[1]
    step = total // 2
    half = jax.ShapeDtypeStruct((4, 3, width // 8, wide), BF)
    out = pl.BlockSpec((4, 1, width // 8, wide), lambda w, k: (0, w, 0, 0))
    return pl.pallas_call(
        weight_gradients_body,
        grid=(3, 2),
        out_shape=(half, half),
        in_specs=[
            pl.BlockSpec(memory_space=pltpu.SMEM),
            pl.BlockSpec((1, width, step), lambda w, k: (w // 2, 0, k)),
            pl.BlockSpec((1, step, wide), lambda w, k: (w, k, 0)),
        ],
        out_specs=(out, out),
        scratch_shapes=[pltpu.VMEM((width, wide), F32)],
        cost_estimate=pl.CostEstimate(
            flops=6 * total * width * wide,
            bytes_accessed=6 * total * (width + wide),
            transcendentals=0,
        ),
        name="weight_gradients",
    )(place, rows_t, units)


def per_device(
    tokens,
    doc_ids,
    w_query,
    b_query,
    key_projection,
    key_bias_vector,
    value_projection,
    value_bias_vector,
    w_output,
    gain_attn,
    gain_mlp,
    w_gate,
    w_up,
    w_down,
    cotangent,
):
    mesh = Mesh()
    token_count, width = tokens.shape
    rows = w_query.shape[0]
    padded = (rows + 5 + 15) // 16 * 16
    query_width = QUERY_HEADS * HEAD_WIDTH
    kv_width = KEY_VALUE_HEADS * HEAD_WIDTH
    kv_rows = key_bias_vector.shape[0]
    fused_width = query_width + 2 * kv_width
    blocks = mesh.shards * mesh.ctxs

    all_width = fused_width + width
    small_vectors = [b_query, key_bias_vector, value_bias_vector, gain_attn, gain_mlp]
    small_counts = [vector.shape[0] for vector in small_vectors]
    packed = jnp.concatenate(
        [jnp.concatenate([w_query, key_projection, value_projection, w_output], 1)]
        + [
            jnp.pad(vector[None], ((0, 0), (0, all_width - vector.shape[0])))
            for vector in small_vectors
        ]
        + [jnp.zeros((padded - rows - len(small_vectors), all_width), BF)],
        0,
    )
    if mesh.fast:
        _, sides, mine, theirs = mesh.gather_spread(packed)
        cosine, sine = rope_tables(mesh.c, token_count)
        fused_weight, output_weight, query_t, own, first_gain, second_gain = project(
            mesh.place(), mine, theirs, tokens, cosine, sine, fused_width
        )
        line = mesh.gather_line(jnp.concatenate([w_gate, w_up, w_down.T], 0), own)
        others = [mesh.across(part) for part in line]
        late, sides = lax.optimization_barrier((cotangent, sides))
        grad_parts = mesh.gather_tokens(late)
    else:
        gathered = lax.all_gather(packed, ("shard", "ctx"), axis=0)
        projection = gathered[:, :rows].reshape(width, all_width)
        smalls = gathered[:, rows:]
        weights = jnp.stack(
            [
                lax.all_gather(part, ("shard", "ctx"), axis=0, tiled=True)
                for part in (w_gate, w_up, w_down.T)
            ]
        )
        grad_parts = mesh.gather_tokens(cotangent)
        fused_weight = projection[:, :fused_width]
        output_weight = projection[:, fused_width:]
        bias_q, bias_k, bias_v, first_gain, second_gain = (
            smalls[:, i, :count].reshape(-1).astype(F32) for i, count in enumerate(small_counts)
        )
        fused_bias = jnp.concatenate([bias_q, bias_k, bias_v])
        tok_float = tokens.astype(F32)
        first_inv = root_inverse(tok_float)
        normed_attn = (tok_float * first_inv * first_gain).astype(BF)
        cosine, sine = rope_tables(mesh.c, token_count)
        fused_t = dot(fused_weight, normed_attn, 0, 1) + fused_bias[:, None]
        query_t = rotate(fused_t[:query_width], cosine, sine).astype(BF) * (HEAD_WIDTH ** (-0.5))
        key_t = rotate(fused_t[query_width : query_width + kv_width], cosine, sine).astype(BF)
        value_t = fused_t[query_width + kv_width :].astype(BF)
        own = jnp.concatenate([key_t, value_t], 0)
        first_gain, second_gain = first_gain[None], second_gain[None]
    other = mesh.across(own)
    half = mesh.c.astype(jnp.int32).reshape(1)
    doc_col = doc_ids.reshape(-1, 1)
    mixed_t, lse = attention_forward(half, doc_ids, doc_col, query_t, own, other)

    hidden, normed_mlp = output_projection(tokens, mixed_t, output_weight, second_gain)
    normed_parts = mesh.gather_tokens(normed_mlp)
    if mesh.fast:
        line, others, _ = lax.optimization_barrier((line, others, normed_mlp))
        weights = assemble_line(mesh.place(), line, others, 3)

    total = token_count * mesh.tps
    backs, downs, kept = [], [], []
    groups = ((0, 1), (1, 3), (3, 4)) if mesh.tps == 4 else ((i, i + 1) for i in range(mesh.tps))
    for index, (low, high) in enumerate(groups):
        some_backs, some_downs, kept = mlp(
            normed_parts[low:high],
            grad_parts[low:high],
            weights,
            kept,
            low * token_count,
            total,
        )
        backs += some_backs
        downs += some_downs
    units, rows_t = kept
    if mesh.fast:
        back_parts = mesh.exchange_tokens(backs)
    else:
        zero = jnp.zeros_like(tokens)
        back_parts = [mesh.scatter_tokens(backs).astype(BF), zero, zero, zero]
    if mesh.fast:
        send, keep = weight_gradients(mesh.place(), units, rows_t)
        part_gate, part_up, part_down = mesh.scatter_line(send, keep)
        downs, back_parts = lax.optimization_barrier((downs, back_parts))
    else:
        part_gate, part_up, part_down = (
            lax.psum_scatter(
                dot(rows_t[i // 2], units[i], 1, 0),
                ("shard", "ctx"),
                scatter_dimension=0,
                tiled=True,
            )
            for i in range(3)
        )
    part_down = part_down.T
    grad_hidden, grad_mixed_t, grad_second_gain = middle(
        back_parts, hidden, cotangent, output_weight, second_gain
    )
    grad_query_rot, own_sums, to_other = attention_backward(
        half, doc_ids, doc_col, query_t, own, other, grad_mixed_t, lse
    )
    hidden_late, grad_query_rot = lax.optimization_barrier((hidden, grad_query_rot))
    result = (hidden_late + mesh.scatter_tokens(downs).astype(F32)).astype(BF)
    received = mesh.across(to_other)
    if mesh.fast:
        grad_tokens, send, keep = projection_gradients(
            mesh.place(),
            grad_query_rot,
            own_sums,
            received,
            cosine,
            sine,
            tokens,
            first_gain,
            grad_second_gain,
            grad_hidden,
            mixed_t,
            fused_weight,
        )
        summed = mesh.reduce_rows(send, keep)
        index = mesh.z * mesh.ctxs + mesh.c

        def own_part(line, start, count):
            return lax.dynamic_slice_in_dim(line, start + index * count, count, 0)

        first, second = summed[rows], summed[rows + 1]
        sum_small = [
            own_part(first, 0, rows),
            own_part(first, query_width, kv_rows),
            own_part(first, query_width + kv_width, kv_rows),
            own_part(first, fused_width, rows),
            own_part(second, 0, rows),
        ]
        return (
            result,
            grad_tokens,
            summed[:rows, :query_width],
            sum_small[0],
            summed[:rows, query_width : query_width + kv_width],
            sum_small[1],
            summed[:rows, query_width + kv_width : fused_width],
            sum_small[2],
            summed[:rows, fused_width:],
            sum_small[3],
            sum_small[4],
            part_gate,
            part_up,
            part_down,
        )
    grad_output_weight = dot(mixed_t, grad_hidden.astype(BF), 1, 0)
    own_sums_t = (own_sums + received).astype(BF).astype(F32)
    grad_query_pre = rotate(grad_query_rot.astype(F32), cosine, -sine)
    grad_key_pre = rotate(own_sums_t[:kv_width], cosine, -sine)
    fused_grad_t = jnp.concatenate([grad_query_pre, grad_key_pre, own_sums_t[kv_width:]], 0)
    grad_fused_bias = jnp.sum(fused_grad_t, 1)
    fused_low = fused_grad_t.astype(BF)
    grad_normed_attn = dot(fused_low, fused_weight, 0, 1)
    grad_fused_weight = dot(normed_attn, fused_low, 0, 1)
    scaled_one = grad_normed_attn * first_gain
    grad_tokens = (
        grad_hidden
        + first_inv * scaled_one
        - tok_float * first_inv**3 * jnp.mean(scaled_one * tok_float, -1, keepdims=True)
    )
    grad_first_gain = jnp.sum(grad_normed_attn * tok_float * first_inv, 0)

    small_sums = [
        grad_fused_bias[:query_width],
        grad_fused_bias[query_width : query_width + kv_width],
        grad_fused_bias[query_width + kv_width :],
        grad_first_gain,
        grad_second_gain[0],
    ]
    grad_packed = jnp.concatenate(
        [
            jnp.concatenate([grad_fused_weight, grad_output_weight], 1).reshape(
                blocks, rows, all_width
            )
        ]
        + [
            jnp.pad(
                vector.reshape(blocks, 1, count), ((0, 0), (0, 0), (0, all_width - count))
            )
            for vector, count in zip(small_sums, small_counts)
        ]
        + [jnp.zeros((blocks, padded - rows - len(small_sums), all_width), F32)],
        1,
    )
    summed = lax.psum_scatter(grad_packed, ("shard", "ctx"), scatter_dimension=0, tiled=True)
    summed = lax.psum(summed[0], "tp")
    sum_small = [summed[rows + i, :count] for i, count in enumerate(small_counts)]
    return (
        result,
        grad_tokens.astype(BF),
        summed[:rows, :query_width],
        sum_small[0],
        summed[:rows, query_width : query_width + kv_width],
        sum_small[1],
        summed[:rows, query_width + kv_width : fused_width],
        sum_small[2],
        summed[:rows, fused_width:],
        sum_small[3],
        sum_small[4],
        part_gate,
        part_up,
        part_down,
    )


def solution(mesh):
    both = ("shard", "ctx")
    every = ("shard", "ctx", "tp")
    in_specs = (
        P(every, None),
        P(("shard", "tp"), None),
        P(both, None),
        P(both),
        P(both, None),
        P(both),
        P(both, None),
        P(both),
        P(both, None),
        P(both),
        P(both),
        P(both, "tp"),
        P(both, "tp"),
        P("tp", both),
        P(every, None),
    )
    out_specs = (
        P(every, None),
        P(every, None),
        P(both, None),
        P(both),
        P(both, None),
        P(both),
        P(both, None),
        P(both),
        P(both, None),
        P(both),
        P(both),
        P(both, "tp"),
        P(both, "tp"),
        P("tp", both),
    )

    step = jax.shard_map(
        per_device, mesh=mesh, in_specs=in_specs, out_specs=out_specs, check_vma=False
    )
    if tuple(mesh.shape[name] for name in every) != (4, 2, 4):
        return step
    return step
```

profile of v0, /device:TPU:0, one launch (start us, length us, event | category | flops | bytes accessed | tf_op | source)
XLA Modules:
  0.0 439.9 jit_solution(2783969998726499800)
XLA Ops:
  4.1 1.1 pad_maximum_fusion.1
  5.7 3.1 collective-permute-start
  8.8 2.6 collective-permute-start.1
  11.4 2.5 collective-permute-done
  13.9 7.8 %collective-permute-done.1 = bf16[32,2048]{1,0:T(8,128)(2,1)S(1)} collective-permute-done((bf16[32,2048]{1,0:T(8,128)(2,1)S(1)}, bf16[32,2048]{1,0:T(8,128)(2,1)S(1)}, u32[]{:S(2)}, u32[]{:S(2)}) %collective-permute-start.1) | collective-permute-done | bytes 131104 | tf_op jit(solution)/shard_map/ppermute | solution.py:269
  21.7 1.6 collective-permute-start.3
  23.3 1.5 collective-permute-start.4
  25.5 8.3 %collective-permute-done.3.refs_2_ = bf16[96,2048]{1,0:T(8,128)(2,1)S(1)} collective-permute-done((bf16[96,2048]{1,0:T(8,128)(2,1)S(1)}, bf16[96,2048]{1,0:T(8,128)(2,1)S(1)}, u32[]{:S(2)}, u32[]{:S(2)}) %collective-permute-start.3) | collective-permute-done | bytes 393248 | tf_op jit(solution)/shard_map/ppermute | solution.py:266
  33.8 6.1 %collective-permute-done.4.refs_3_ = bf16[96,2048]{1,0:T(8,128)(2,1)S(1)} collective-permute-done((bf16[96,2048]{1,0:T(8,128)(2,1)S(1)}, bf16[96,2048]{1,0:T(8,128)(2,1)S(1)}, u32[]{:S(2)}, u32[]{:S(2)}) %collective-permute-start.4) | collective-permute-done | bytes 393248 | tf_op jit(solution)/shard_map/ppermute | solution.py:266
  40.4 4.6 %collective-permute-start.13 = (bf16[336,1216]{1,0:T(8,128)(2,1)S(1)}, bf16[336,1216]{1,0:T(8,128)(2,1)S(1)}, u32[]{:S(2)}, u32[]{:S(2)}) collective-permute-start(bf16[336,1216]{1,0:T(8,128)(2,1)S(1)} %pad_maximum_fusion.refs_0_), channel_id=1, source_target_pairs={{0,16},{8,24},{16,0},{24,8},{1,17},{9,25},{17,1},{25,9},{2,18},{10... | collective-permute-start | bytes 2451464 | tf_op jit(solution)/shard_map/ppermute | solution.py:269
  46.6 7.3 %project.1 = (bf16[896,1152]{1,0:T(8,128)(2,1)}, bf16[896,896]{1,0:T(8,128)(2,1)}, bf16[896,512]{1,0:T(8,128)(2,1)}, bf16[256,512]{1,0:T(8,128)(2,1)}, f32[1,896]{1,0:T(1,128)}, /*index=5*/f32[1,896]{1,0:T(1,128)}) custom-call(s32[3]{0:T(128)} %pad_add_fusion.place, bf16[128,2048]{1,0:T(8,128)(2,1)} %copy-done.13, bf16[96,2048]{1,0:T(8,128)(2,1)} %copy-done.17, ...), custom_call_target="tpu_custom_call" | custom-call | flops 3000000000 | bytes 12000000 | tf_op jit(solution)/shard_map/project/pallas_call | solution.py:435
  53.9 1.7 copy.33.doc_col
  55.6 1.0 collective-permute-start.22
  56.7 1.0 collective-permute-start.23
  57.7 25.1 %collective-permute-done.13.refs_2_ = bf16[336,1216]{1,0:T(8,128)(2,1)S(1)} collective-permute-done((bf16[336,1216]{1,0:T(8,128)(2,1)S(1)}, bf16[336,1216]{1,0:T(8,128)(2,1)S(1)}, u32[]{:S(2)}, u32[]{:S(2)}) %collective-permute-start.13) | collective-permute-done | bytes 817184 | tf_op jit(solution)/shard_map/ppermute | solution.py:269
  83.5 1.3 collective-permute-start.15
  84.8 15.7 %attention_forward.1 = (bf16[896,512]{1,0:T(8,128)(2,1)}, f32[14,8,512]{2,1,0:T(8,128)}) custom-call(s32[1]{0:T(128)} %bitcast.half_ref, s32[1,1024]{1,0:T(1,128)} %doc_row.3, s32[1024,1]{1,0:T(8,128)} %copy.33.doc_col, bf16[896,512]{1,0:T(8,128)(2,1)} %get-tuple-element.84.query_t, bf16[256,512]{1,0:T(8,128)(2,1)} %get-tuple-element.85.own, ...), custom_call_target="tpu_custom_call" | custom-call | flops 15000000512 | bytes 1835008 | tf_op jit(solution)/shard_map/attention_forward/pallas_call | solution.py:111
  100.5 4.8 %output_projection.1 = (f32[512,896]{1,0:T(8,128)}, bf16[512,896]{1,0:T(8,128)(2,1)}) custom-call(bf16[512,896]{1,0:T(8,128)(2,1)} %tokens.3, bf16[896,512]{1,0:T(8,128)(2,1)} %get-tuple-element.86.mixed_t, bf16[896,896]{1,0:T(8,128)(2,1)} %get-tuple-element.87.weight, f32[1,896]{1,0:T(1,128)} %get-tuple-element.88.gain), custom_call_target="tpu_custom_call" | custom-call | flops 1000000000 | bytes 6000000 | tf_op jit(solution)/shard_map/output_projection/pallas_call | solution.py:468
  105.2 1.3 collective-permute-start.20
  106.5 3.5 collective-permute-start.12
  110.8 1.2 broadcast_select_fusion.refs_3_
  112.1 13.1 %collective-permute-done.12.refs_1_ = bf16[336,1216]{1,0:T(8,128)(2,1)} collective-permute-done((bf16[336,1216]{1,0:T(8,128)(2,1)S(1)}, bf16[336,1216]{1,0:T(8,128)(2,1)}, u32[]{:S(2)}, u32[]{:S(2)}) %collective-permute-start.12) | collective-permute-done | bytes 817184 | tf_op jit(solution)/shard_map/ppermute | solution.py:269
  125.2 4.8 %collective-permute-start.16 = (bf16[336,1216]{1,0:T(8,128)(2,1)S(1)}, bf16[336,1216]{1,0:T(8,128)(2,1)S(1)}, u32[]{:S(2)}, u32[]{:S(2)}) collective-permute-start(bf16[336,1216]{1,0:T(8,128)(2,1)S(1)} %pad_maximum_fusion.refs_0_), channel_id=1, source_target_pairs={{0,4},{4,0},{1,5},{5,1},{2,6},{6,2},{3,7},{7,3},{8,12},{12,8},{9,1... | collective-permute-start | bytes 2451464 | tf_op jit(solution)/shard_map/ppermute | solution.py:263
  130.5 1.7 collective-permute-start.25
  132.3 1.4 collective-permute-start.24
  134.6 1.2 collective-permute-done.19.refs_7_
  135.8 6.7 %assemble_line.1.refs_2_.refs_3_.refs_4_.refs_5_.refs_6_ = bf16[3,896,1216]{2,1,0:T(8,128)(2,1)} custom-call(s32[3]{0:T(128)} %pad_add_fusion.place, bf16[336,1216]{1,0:T(8,128)(2,1)} %copy-done.2, bf16[336,1216]{1,0:T(8,128)(2,1)} %collective-permute-done.12.refs_1_, bf16[336,1216]{1,0:T(8,128)(2,1)} %copy-done.11, bf16[336,1216]{1,0:T(8,128)(2,1)} %copy-done.3, ...), custom_call_target="tpu_custom_call" | custom-call | bytes 13074432 | tf_op jit(solution)/shard_map/assemble_line/pallas_call | solution.py:588
  142.5 14.2 %mlp.3 = (bf16[512,896]{1,0:T(8,128)(2,1)}, bf16[512,896]{1,0:T(8,128)(2,1)}, bf16[3,2048,1216]{2,1,0:T(8,128)(2,1)}, bf16[2,896,2048]{2,1,0:T(8,128)(2,1)}) custom-call(bf16[512,896]{1,0:T(8,128)(2,1)} %get-tuple-element.111.refs_0_, bf16[512,896]{1,0:T(8,128)(2,1)} %cotangent.1, bf16[3,896,1216]{2,1,0:T(8,128)(2,1)} %assemble_line.1.refs_2_.refs_3_.refs_4_.refs_5_.refs_6_, ...), custom_call_target="tpu_custom_call" | custom-call | flops 6694109184 | bytes 15187968 | tf_op jit(solution)/shard_map/mlp/pallas_call | solution.py:768
  156.7 25.9 %mlp.4 = (bf16[512,896]{1,0:T(8,128)(2,1)}, bf16[512,896]{1,0:T(8,128)(2,1)}, bf16[512,896]{1,0:T(8,128)(2,1)}, bf16[512,896]{1,0:T(8,128)(2,1)}, bf16[3,2048,12...) custom-call(bf16[512,896]{1,0:T(8,128)(2,1)} %collective-permute-done.20.refs_0_, ...), custom_call_target="tpu_custom_call", output_to_operand_aliasing={{4}: (7, {}), {5}: (8, {})} | custom-call | flops 13388218368 | bytes 23838720 | tf_op jit(solution)/shard_map/mlp/pallas_call | solution.py:768
  183.4 1.5 collective-permute-start.27
  185.0 14.4 %mlp.5 = (bf16[512,896]{1,0:T(8,128)(2,1)}, bf16[512,896]{1,0:T(8,128)(2,1)}, bf16[3,2048,1216]{2,1,0:T(8,128)(2,1)}, bf16[2,896,2048]{2,1,0:T(8,128)(2,1)}) custom-call(bf16[512,896]{1,0:T(8,128)(2,1)} %collective-permute-done.24.refs_0_, bf16[512,896]{1,0:T(8,128)(2,1)} %collective-permute-done.25.refs_1_, ...), custom_call_target="tpu_custom_call", output_to_operand_aliasing={{2}: (5, {}), {3}: (6, {})} | custom-call | flops 6694109184 | bytes 15187968 | tf_op jit(solution)/shard_map/mlp/pallas_call | solution.py:768
  199.3 1.2 collective-permute-start.28
  200.6 5.5 %collective-permute-done.26.one = bf16[512,896]{1,0:T(8,128)(2,1)S(1)} collective-permute-done((bf16[512,896]{1,0:T(8,128)(2,1)}, bf16[512,896]{1,0:T(8,128)(2,1)S(1)}, u32[]{:S(2)}, u32[]{:S(2)}) %collective-permute-start.26) | collective-permute-done | bytes 917536 | tf_op jit(solution)/shard_map/ppermute | solution.py:266
  206.1 19.6 %collective-permute-done.27.two = bf16[512,896]{1,0:T(8,128)(2,1)S(1)} collective-permute-done((bf16[512,896]{1,0:T(8,128)(2,1)}, bf16[512,896]{1,0:T(8,128)(2,1)S(1)}, u32[]{:S(2)}, u32[]{:S(2)}) %collective-permute-start.27) | collective-permute-done | bytes 917536 | tf_op jit(solution)/shard_map/ppermute | solution.py:266
  227.0 6.5 %middle.1 = (f32[512,896]{1,0:T(8,128)}, bf16[896,512]{1,0:T(8,128)(2,1)}, f32[1,896]{1,0:T(1,128)}) custom-call(bf16[512,896]{1,0:T(8,128)(2,1)} %get-tuple-element.120.own, bf16[512,896]{1,0:T(8,128)(2,1)} %copy-done.7, bf16[512,896]{1,0:T(8,128)(2,1)} %copy-done.8, bf16[512,896]{1,0:T(8,128)(2,1)} %copy-done.9, f32[512,896]{1,0:T(8,128)} %get-tuple-element.127.hidden, ...), custom_call_target="tpu_custom_call" | custom-call | flops 1000000000 | bytes 9000000 | tf_op jit(solution)/shard_map/middle/pallas_call | solution.py:500
  233.4 18.9 %attention_backward.1 = (bf16[896,512]{1,0:T(8,128)(2,1)}, f32[256,512]{1,0:T(8,128)}, f32[256,512]{1,0:T(8,128)}) custom-call(s32[1]{0:T(128)} %bitcast.half_ref, s32[1,1024]{1,0:T(1,128)} %doc_row.3, s32[1024,1]{1,0:T(8,128)} %copy.33.doc_col, bf16[896,512]{1,0:T(8,128)(2,1)} %get-tuple-element.84.query_t, bf16[256,512]{1,0:T(8,128)(2,1)} %get-tuple-element.85.own, ...), custom_call_target="tpu_custom_call" | custom-call | flops 35000000512 | bytes 3670016 | tf_op jit(solution)/shard_map/attention_backward/pallas_call | solution.py:213
  252.3 9.5 %collective-permute-start.32 = (f32[256,512]{1,0:T(8,128)}, f32[256,512]{1,0:T(8,128)}, u32[]{:S(2)}, u32[]{:S(2)}) collective-permute-start(f32[256,512]{1,0:T(8,128)} %get-tuple-element.134), channel_id=1, source_target_pairs={{0,4},{4,0},{1,5},{5,1},{2,6},{6,2},{3,7},{7,3},{8,12},{12,8},{9,1... | collective-permute-start | bytes 1572872 | tf_op jit(solution)/shard_map/ppermute | solution.py:263
  261.8 23.0 %weight_gradients.1 = (bf16[4,3,112,1216]{3,2,1,0:T(8,128)(2,1)}, bf16[4,3,112,1216]{3,2,1,0:T(8,128)(2,1)}) custom-call(s32[3]{0:T(128)} %pad_add_fusion.place, bf16[2,896,2048]{2,1,0:T(8,128)(2,1)} %get-tuple-element.146.left, bf16[3,2048,1216]{2,1,0:T(8,128)(2,1)} %get-tuple-element.147.right), custom_call_target="tpu_custom_call" | custom-call | flops 13388218368 | bytes 25952256 | tf_op jit(solution)/shard_map/weight_gradients/pallas_call | solution.py:828
  284.8 11.1 %projection_gradients.1 = (bf16[512,896]{1,0:T(8,128)(2,1)}, bf16[4,128,2048]{2,1,0:T(8,128)(2,1)}, bf16[4,128,2048]{2,1,0:T(8,128)(2,1)}) custom-call(s32[3]{0:T(128)} %pad_add_fusion.place, bf16[896,512]{1,0:T(8,128)(2,1)} %get-tuple-element.132.grad_query, f32[256,512]{1,0:T(8,128)} %get-tuple-element.133.own_sums, ...), custom_call_target="tpu_custom_call" | custom-call | flops 6000000000 | bytes 16000000 | tf_op jit(solution)/shard_map/projection_gradients/pallas_call | solution.py:692
  296.4 1.4 collective-permute-start.31
  297.9 1.5 collective-permute-start.30
  300.6 4.5 %fold.1 = (f32[4,32,2048]{2,1,0:T(8,128)}, bf16[4,32,2048]{2,1,0:T(8,128)(2,1)}, bf16[4,32,2048]{2,1,0:T(8,128)(2,1)}, bf16[4,32,2048]{2,1,0:T(8,128)(2,1)}) custom-call(s32[3]{0:T(128)} %pad_add_fusion.place, bf16[4,128,2048]{2,1,0:T(8,128)(2,1)} %get-tuple-element.140.keep, bf16[4,128,2048]{2,1,0:T(8,128)(2,1)} %collective-permute-done.33.received), custom_call_target="tpu_custom_call" | custom-call | bytes 6291456 | tf_op jit(solution)/shard_map/fold/pallas_call | solution.py:528
  305.1 1.4 collective-permute-start.36
  306.5 14.4 %collective-permute-done.31 = bf16[512,896]{1,0:T(8,128)(2,1)} collective-permute-done((bf16[512,896]{1,0:T(8,128)(2,1)}, bf16[512,896]{1,0:T(8,128)(2,1)}, u32[]{:S(2)}, u32[]{:S(2)}) %collective-permute-start.31) | collective-permute-done | bytes 917536 | tf_op jit(solution)/shard_map/ppermute | solution.py:266
  320.9 1.2 collective-permute-start.35
  323.9 6.8 %fold_line.1 = (f32[3,112,1216]{2,1,0:T(8,128)}, bf16[3,112,1216]{2,1,0:T(8,128)(2,1)}, bf16[3,112,1216]{2,1,0:T(8,128)(2,1)}, bf16[3,112,1216]{2,1,0:T(8,128)(2,1)}) custom-call(s32[3]{0:T(128)} %pad_add_fusion.place, bf16[4,3,112,1216]{3,2,1,0:T(8,128)(2,1)} %get-tuple-element.148.keep, bf16[4,3,112,1216]{3,2,1,0:T(8,128)(2,1)} %copy-done.1), custom_call_target="tpu_custom_call" | custom-call | bytes 9805824 | tf_op jit(solution)/shard_map/fold_line/pallas_call | solution.py:555
  330.6 10.0 %collective-permute-done.30 = bf16[512,896]{1,0:T(8,128)(2,1)} collective-permute-done((bf16[512,896]{1,0:T(8,128)(2,1)}, bf16[512,896]{1,0:T(8,128)(2,1)}, u32[]{:S(2)}, u32[]{:S(2)}) %collective-permute-start.30) | collective-permute-done | bytes 917536 | tf_op jit(solution)/shard_map/ppermute | solution.py:266
  340.6 2.0 collective-permute-start.46
  342.7 1.1 collective-permute-start.45
  343.8 8.0 %collective-permute-done.36 = bf16[4,32,2048]{2,1,0:T(8,128)(2,1)} collective-permute-done((bf16[4,32,2048]{2,1,0:T(8,128)(2,1)}, bf16[4,32,2048]{2,1,0:T(8,128)(2,1)}, u32[]{:S(2)}, u32[]{:S(2)}) %collective-permute-start.36) | collective-permute-done | bytes 524320 | tf_op jit(solution)/shard_map/ppermute | solution.py:266
  351.9 1.7 collective-permute-start.44
  353.6 3.2 add_convert_fusion
  356.7 5.3 %collective-permute-done.35 = bf16[4,32,2048]{2,1,0:T(8,128)(2,1)} collective-permute-done((bf16[4,32,2048]{2,1,0:T(8,128)(2,1)}, bf16[4,32,2048]{2,1,0:T(8,128)(2,1)}, u32[]{:S(2)}, u32[]{:S(2)}) %collective-permute-start.35) | collective-permute-done | bytes 524320 | tf_op jit(solution)/shard_map/ppermute | solution.py:266
  362.1 1.8 convert_add_fusion.1
  363.9 2.1 collective-permute-start.39
  366.0 2.4 collective-permute-start.37
  368.4 14.1 %collective-permute-done.45 = bf16[3,112,1216]{2,1,0:T(8,128)(2,1)S(1)} collective-permute-done((bf16[3,112,1216]{2,1,0:T(8,128)(2,1)}, bf16[3,112,1216]{2,1,0:T(8,128)(2,1)S(1)}, u32[]{:S(2)}, u32[]{:S(2)}) %collective-permute-start.45) | collective-permute-done | bytes 817184 | tf_op jit(solution)/shard_map/ppermute | solution.py:269
  382.6 42.7 %collective-permute-done.44 = bf16[3,112,1216]{2,1,0:T(8,128)(2,1)S(1)} collective-permute-done((bf16[3,112,1216]{2,1,0:T(8,128)(2,1)}, bf16[3,112,1216]{2,1,0:T(8,128)(2,1)S(1)}, u32[]{:S(2)}, u32[]{:S(2)}) %collective-permute-start.44) | collective-permute-done | bytes 817184 | tf_op jit(solution)/shard_map/ppermute | solution.py:269
  425.6 2.4 collective-permute-done.38
  428.1 1.5 collective-permute-start.40
  429.6 1.5 collective-permute-start.41
  431.7 1.2 slice_bitcast_fusion
  432.9 1.2 collective-permute-done.40
  434.2 1.3 collective-permute-done.41
  (118 shorter events, 20.4 us)
Async XLA Ops:
  0.6 24.6 %copy-start.14 = (bf16[1216,112]{0,1:T(8,128)(2,1)S(1)}, bf16[1216,112]{0,1:T(8,128)(2,1)}, u32[]{:S(2)}) copy-start(bf16[1216,112]{0,1:T(8,128)(2,1)} %param.28) | copy-start | bytes 817156
  0.7 24.6 %copy-start.15 = (bf16[112,1216]{1,0:T(8,128)(2,1)S(1)}, bf16[112,1216]{1,0:T(8,128)(2,1)}, u32[]{:S(2)}) copy-start(bf16[112,1216]{1,0:T(8,128)(2,1)} %param.27) | copy-start | bytes 817156
  0.7 24.6 %copy-start.16 = (bf16[112,1216]{1,0:T(8,128)(2,1)S(1)}, bf16[112,1216]{1,0:T(8,128)(2,1)}, u32[]{:S(2)}) copy-start(bf16[112,1216]{1,0:T(8,128)(2,1)} %param.26) | copy-start | bytes 817156
  5.6 40.9 %copy-start.13 = (bf16[128,2048]{1,0:T(8,128)(2,1)}, bf16[128,2048]{1,0:T(8,128)(2,1)S(1)}, u32[]{:S(2)}) copy-start(bf16[128,2048]{1,0:T(8,128)(2,1)S(1)} %concatenate.16.refs_0_) | copy-start | bytes 1572868
  5.7 8.2 %collective-permute-start = (bf16[32,2048]{1,0:T(8,128)(2,1)S(1)}, bf16[32,2048]{1,0:T(8,128)(2,1)S(1)}, u32[]{:S(2)}, u32[]{:S(2)}) collective-permute-start(bf16[32,2048]{1,0:T(8,128)(2,1)S(1)} %constant_dynamic-slice_fusion.4), channel_id=1, source_target_pairs={{0,8},{8,0},{16,24},{24,16},{1,9},{9,1},{17,25},{25,17},{2,10},{10... | collective-permute-start | bytes 393224 | tf_op jit(solution)/shard_map/ppermute | solution.py:269
  8.8 12.9 %collective-permute-start.1 = (bf16[32,2048]{1,0:T(8,128)(2,1)S(1)}, bf16[32,2048]{1,0:T(8,128)(2,1)S(1)}, u32[]{:S(2)}, u32[]{:S(2)}) collective-permute-start(bf16[32,2048]{1,0:T(8,128)(2,1)S(1)} %constant_dynamic-slice_fusion.4), channel_id=1, source_target_pairs={{0,16},{8,24},{16,0},{24,8},{1,17},{9,25},{17,1},{25,9},{2,18},{10... | collective-permute-start | bytes 393224 | tf_op jit(solution)/shard_map/ppermute | solution.py:269
  11.4 10.3 %collective-permute-start.2 = (bf16[32,2048]{1,0:T(8,128)(2,1)S(1)}, bf16[32,2048]{1,0:T(8,128)(2,1)S(1)}, u32[]{:S(2)}, u32[]{:S(2)}) collective-permute-start(bf16[32,2048]{1,0:T(8,128)(2,1)S(1)} %constant_dynamic-slice_fusion.4), channel_id=1, source_target_pairs={{0,24},{8,16},{16,8},{24,0},{1,25},{9,17},{17,9},{25,1},{2,26},{10... | collective-permute-start | bytes 393224 | tf_op jit(solution)/shard_map/ppermute | solution.py:269
  11.4 29.0 %collective-permute-start.6 = (bf16[128,2048]{1,0:T(8,128)(2,1)S(1)}, bf16[128,2048]{1,0:T(8,128)(2,1)}, u32[]{:S(2)}, u32[]{:S(2)}) collective-permute-start(bf16[128,2048]{1,0:T(8,128)(2,1)S(1)} %concatenate.16.refs_0_), channel_id=1, source_target_pairs={{0,4},{4,0},{1,5},{5,1},{2,6},{6,2},{3,7},{7,3},{8,12},{12,8},{9,1... | collective-permute-start | bytes 1572872 | tf_op jit(solution)/shard_map/ppermute | solution.py:263
  21.7 24.9 %copy-start.17 = (bf16[96,2048]{1,0:T(8,128)(2,1)}, bf16[96,2048]{1,0:T(8,128)(2,1)S(1)}, u32[]{:S(2)}) copy-start(bf16[96,2048]{1,0:T(8,128)(2,1)S(1)} %constant_dynamic-update-slice_fusion.refs_1_) | copy-start | bytes 1179652
  21.7 12.1 %collective-permute-start.3 = (bf16[96,2048]{1,0:T(8,128)(2,1)S(1)}, bf16[96,2048]{1,0:T(8,128)(2,1)S(1)}, u32[]{:S(2)}, u32[]{:S(2)}) collective-permute-start(bf16[96,2048]{1,0:T(8,128)(2,1)S(1)} %constant_dynamic-update-slice_fusion.refs_1_), channel_id=1, source_target_pairs={{0,1},{1,0},{2,3},{3,2},{4,5},{5,4},{6,7},{7,6},{8,9},{9,8},{10,11... | collective-permute-start | bytes 1179656 | tf_op jit(solution)/shard_map/ppermute | solution.py:266
  23.3 16.6 %collective-permute-start.4 = (bf16[96,2048]{1,0:T(8,128)(2,1)S(1)}, bf16[96,2048]{1,0:T(8,128)(2,1)S(1)}, u32[]{:S(2)}, u32[]{:S(2)}) collective-permute-start(bf16[96,2048]{1,0:T(8,128)(2,1)S(1)} %constant_dynamic-update-slice_fusion.refs_1_), channel_id=1, source_target_pairs={{0,2},{1,3},{2,0},{3,1},{4,6},{5,7},{6,4},{7,5},{8,10},{9,11},{10,... | collective-permute-start | bytes 1179656 | tf_op jit(solution)/shard_map/ppermute | solution.py:266
  24.8 15.1 %collective-permute-start.5 = (bf16[96,2048]{1,0:T(8,128)(2,1)S(1)}, bf16[96,2048]{1,0:T(8,128)(2,1)}, u32[]{:S(2)}, u32[]{:S(2)}) collective-permute-start(bf16[96,2048]{1,0:T(8,128)(2,1)S(1)} %constant_dynamic-update-slice_fusion.refs_1_), channel_id=1, source_target_pairs={{0,3},{1,2},{2,1},{3,0},{4,7},{5,6},{6,5},{7,4},{8,11},{9,10},{10,... | collective-permute-start | bytes 1179656 | tf_op jit(solution)/shard_map/ppermute | solution.py:266
  25.4 99.8 %copy-start.2 = (bf16[336,1216]{1,0:T(8,128)(2,1)}, bf16[336,1216]{1,0:T(8,128)(2,1)S(1)}, u32[]{:S(2)}) copy-start(bf16[336,1216]{1,0:T(8,128)(2,1)S(1)} %pad_maximum_fusion.refs_0_) | copy-start | bytes 2451460
  25.4 21.1 %collective-permute-start.7 = (bf16[96,2048]{1,0:T(8,128)(2,1)S(1)}, bf16[96,2048]{1,0:T(8,128)(2,1)}, u32[]{:S(2)}, u32[]{:S(2)}) collective-permute-start(bf16[96,2048]{1,0:T(8,128)(2,1)S(1)} %constant_dynamic-update-slice_fusion.refs_1_), channel_id=1, source_target_pairs={{0,4},{4,0},{1,5},{5,1},{2,6},{6,2},{3,7},{7,3},{8,12},{12,8},{9,1... | collective-permute-start | bytes 1179656 | tf_op jit(solution)/shard_map/ppermute | solution.py:263
  33.8 12.8 %copy-start.19 = (bf16[96,2048]{1,0:T(8,128)(2,1)}, bf16[96,2048]{1,0:T(8,128)(2,1)S(1)}, u32[]{:S(2)}) copy-start(bf16[96,2048]{1,0:T(8,128)(2,1)S(1)} %collective-permute-done.3.refs_2_) | copy-start | bytes 1179652
  33.8 12.7 %collective-permute-start.8 = (bf16[96,2048]{1,0:T(8,128)(2,1)S(1)}, bf16[96,2048]{1,0:T(8,128)(2,1)}, u32[]{:S(2)}, u32[]{:S(2)}) collective-permute-start(bf16[96,2048]{1,0:T(8,128)(2,1)S(1)} %collective-permute-done.3.refs_2_), channel_id=1, source_target_pairs={{0,4},{4,0},{1,5},{5,1},{2,6},{6,2},{3,7},{7,3},{8,12},{12,8},{9,1... | collective-permute-start | bytes 1179656 | tf_op jit(solution)/shard_map/ppermute | solution.py:263
  39.9 6.7 %copy-start.20 = (bf16[96,2048]{1,0:T(8,128)(2,1)}, bf16[96,2048]{1,0:T(8,128)(2,1)S(1)}, u32[]{:S(2)}) copy-start(bf16[96,2048]{1,0:T(8,128)(2,1)S(1)} %collective-permute-done.4.refs_3_) | copy-start | bytes 1179652
  39.9 6.7 %collective-permute-start.9 = (bf16[96,2048]{1,0:T(8,128)(2,1)S(1)}, bf16[96,2048]{1,0:T(8,128)(2,1)}, u32[]{:S(2)}, u32[]{:S(2)}) collective-permute-start(bf16[96,2048]{1,0:T(8,128)(2,1)S(1)} %collective-permute-done.4.refs_3_), channel_id=1, source_target_pairs={{0,4},{4,0},{1,5},{5,1},{2,6},{6,2},{3,7},{7,3},{8,12},{12,8},{9,1... | collective-permute-start | bytes 1179656 | tf_op jit(solution)/shard_map/ppermute | solution.py:263
  39.9 6.7 %collective-permute-start.10 = (bf16[96,2048]{1,0:T(8,128)(2,1)}, bf16[96,2048]{1,0:T(8,128)(2,1)}, u32[]{:S(2)}, u32[]{:S(2)}) collective-permute-start(bf16[96,2048]{1,0:T(8,128)(2,1)} %collective-permute-done.5.refs_4_), channel_id=1, source_target_pairs={{0,4},{4,0},{1,5},{5,1},{2,6},{6,2},{3,7},{7,3},{8,12},{12,8},{9,1... | collective-permute-start | bytes 1179656 | tf_op jit(solution)/shard_map/ppermute | solution.py:263
  40.4 42.4 %collective-permute-start.13 = (bf16[336,1216]{1,0:T(8,128)(2,1)S(1)}, bf16[336,1216]{1,0:T(8,128)(2,1)S(1)}, u32[]{:S(2)}, u32[]{:S(2)}) collective-permute-start(bf16[336,1216]{1,0:T(8,128)(2,1)S(1)} %pad_maximum_fusion.refs_0_), channel_id=1, source_target_pairs={{0,16},{8,24},{16,0},{24,8},{1,17},{9,25},{17,1},{25,9},{2,18},{10... | collective-permute-start | bytes 2451464 | tf_op jit(solution)/shard_map/ppermute | solution.py:269
  46.6 9.1 %copy-start.6 = (bf16[512,896]{1,0:T(8,128)(2,1)S(1)}, bf16[512,896]{1,0:T(8,128)(2,1)}, u32[]{:S(2)}) copy-start(bf16[512,896]{1,0:T(8,128)(2,1)} %cotangent.1) | copy-start | bytes 2752516
  53.9 30.9 %collective-permute-start.11 = (bf16[256,512]{1,0:T(8,128)(2,1)}, bf16[256,512]{1,0:T(8,128)(2,1)}, u32[]{:S(2)}, u32[]{:S(2)}) collective-permute-start(bf16[256,512]{1,0:T(8,128)(2,1)} %get-tuple-element.85.own), channel_id=1, source_target_pairs={{0,4},{4,0},{1,5},{5,1},{2,6},{6,2},{3,7},{7,3},{8,12},{12,8},{9,1... | collective-permute-start | bytes 786440 | tf_op jit(solution)/shard_map/ppermute | solution.py:263
  55.6 74.3 %collective-permute-start.22 = (bf16[512,896]{1,0:T(8,128)(2,1)S(1)}, bf16[512,896]{1,0:T(8,128)(2,1)}, u32[]{:S(2)}, u32[]{:S(2)}) collective-permute-start(bf16[512,896]{1,0:T(8,128)(2,1)S(1)} %copy-done.6), channel_id=1, source_target_pairs={{0,1},{1,0},{2,3},{3,2},{4,5},{5,4},{6,7},{7,6},{8,9},{9,8},{10,11... | collective-permute-start | bytes 2752520 | tf_op jit(solution)/shard_map/ppermute | solution.py:266
  56.7 73.4 %collective-permute-start.23 = (bf16[512,896]{1,0:T(8,128)(2,1)S(1)}, bf16[512,896]{1,0:T(8,128)(2,1)}, u32[]{:S(2)}, u32[]{:S(2)}) collective-permute-start(bf16[512,896]{1,0:T(8,128)(2,1)S(1)} %copy-done.6), channel_id=1, source_target_pairs={{0,2},{1,3},{2,0},{3,1},{4,6},{5,7},{6,4},{7,5},{8,10},{9,11},{10,... | collective-permute-start | bytes 2752520 | tf_op jit(solution)/shard_map/ppermute | solution.py:266
  82.8 17.7 %copy-start.11 = (bf16[336,1216]{1,0:T(8,128)(2,1)}, bf16[336,1216]{1,0:T(8,128)(2,1)S(1)}, u32[]{:S(2)}) copy-start(bf16[336,1216]{1,0:T(8,128)(2,1)S(1)} %collective-permute-done.13.refs_2_) | copy-start | bytes 2451460
  82.8 23.7 %collective-permute-start.14 = (bf16[336,1216]{1,0:T(8,128)(2,1)S(1)}, bf16[336,1216]{1,0:T(8,128)(2,1)S(1)}, u32[]{:S(2)}, u32[]{:S(2)}) collective-permute-start(bf16[336,1216]{1,0:T(8,128)(2,1)S(1)} %pad_maximum_fusion.refs_0_), channel_id=1, source_target_pairs={{8,16},{16,8},{9,17},{17,9},{10,18},{18,10},{11,19},{19,11},{12,20... | collective-permute-start | bytes 2451464 | tf_op jit(solution)/shard_map/ppermute | solution.py:293
  83.5 26.6 %collective-permute-start.15 = (bf16[336,1216]{1,0:T(8,128)(2,1)S(1)}, bf16[336,1216]{1,0:T(8,128)(2,1)}, u32[]{:S(2)}, u32[]{:S(2)}) collective-permute-start(bf16[336,1216]{1,0:T(8,128)(2,1)S(1)} %collective-permute-done.13.refs_2_), channel_id=1, source_target_pairs={{16,24},{8,0},{17,25},{9,1},{18,26},{10,2},{19,27},{11,3},{20,28},... | collective-permute-start | bytes 2451464 | tf_op jit(solution)/shard_map/ppermute | solution.py:294
  105.2 25.2 %collective-permute-start.20 = (bf16[512,896]{1,0:T(8,128)(2,1)}, bf16[512,896]{1,0:T(8,128)(2,1)}, u32[]{:S(2)}, u32[]{:S(2)}) collective-permute-start(bf16[512,896]{1,0:T(8,128)(2,1)} %get-tuple-element.111.refs_0_), channel_id=1, source_target_pairs={{0,1},{1,0},{2,3},{3,2},{4,5},{5,4},{6,7},{7,6},{8,9},{9,8},{10,11... | collective-permute-start | bytes 2752520 | tf_op jit(solution)/shard_map/ppermute | solution.py:266
  106.5 18.7 %collective-permute-start.12 = (bf16[336,1216]{1,0:T(8,128)(2,1)S(1)}, bf16[336,1216]{1,0:T(8,128)(2,1)}, u32[]{:S(2)}, u32[]{:S(2)}) collective-permute-start(bf16[336,1216]{1,0:T(8,128)(2,1)S(1)} %pad_maximum_fusion.refs_0_), channel_id=1, source_target_pairs={{0,8},{8,0},{16,24},{24,16},{1,9},{9,1},{17,25},{25,17},{2,10},{10... | collective-permute-start | bytes 2451464 | tf_op jit(solution)/shard_map/ppermute | solution.py:269
  110.0 20.5 %collective-permute-start.21 = (bf16[512,896]{1,0:T(8,128)(2,1)}, bf16[512,896]{1,0:T(8,128)(2,1)S(1)}, u32[]{:S(2)}, u32[]{:S(2)}) collective-permute-start(bf16[512,896]{1,0:T(8,128)(2,1)} %get-tuple-element.111.refs_0_), channel_id=1, source_target_pairs={{0,2},{1,3},{2,0},{3,1},{4,6},{5,7},{6,4},{7,5},{8,10},{9,11},{10,... | collective-permute-start | bytes 2752520 | tf_op jit(solution)/shard_map/ppermute | solution.py:266
  112.1 23.7 %copy-start.3 = (bf16[336,1216]{1,0:T(8,128)(2,1)}, bf16[336,1216]{1,0:T(8,128)(2,1)S(1)}, u32[]{:S(2)}) copy-start(bf16[336,1216]{1,0:T(8,128)(2,1)S(1)} %broadcast_select_fusion.refs_3_) | copy-start | bytes 2451460
  125.2 7.1 %collective-permute-start.16 = (bf16[336,1216]{1,0:T(8,128)(2,1)S(1)}, bf16[336,1216]{1,0:T(8,128)(2,1)S(1)}, u32[]{:S(2)}, u32[]{:S(2)}) collective-permute-start(bf16[336,1216]{1,0:T(8,128)(2,1)S(1)} %pad_maximum_fusion.refs_0_), channel_id=1, source_target_pairs={{0,4},{4,0},{1,5},{5,1},{2,6},{6,2},{3,7},{7,3},{8,12},{12,8},{9,1... | collective-permute-start | bytes 2451464 | tf_op jit(solution)/shard_map/ppermute | solution.py:263
  129.9 4.6 %collective-permute-start.18 = (bf16[336,1216]{1,0:T(8,128)(2,1)}, bf16[336,1216]{1,0:T(8,128)(2,1)}, u32[]{:S(2)}, u32[]{:S(2)}) collective-permute-start(bf16[336,1216]{1,0:T(8,128)(2,1)} %copy-done.11), channel_id=1, source_target_pairs={{0,4},{4,0},{1,5},{5,1},{2,6},{6,2},{3,7},{7,3},{8,12},{12,8},{9,1... | collective-permute-start | bytes 2451464 | tf_op jit(solution)/shard_map/ppermute | solution.py:263
  130.0 4.5 %collective-permute-start.17 = (bf16[336,1216]{1,0:T(8,128)(2,1)}, bf16[336,1216]{1,0:T(8,128)(2,1)}, u32[]{:S(2)}, u32[]{:S(2)}) collective-permute-start(bf16[336,1216]{1,0:T(8,128)(2,1)} %collective-permute-done.12.refs_1_), channel_id=1, source_target_pairs={{0,4},{4,0},{1,5},{5,1},{2,6},{6,2},{3,7},{7,3},{8,12},{12,8},{9,1... | collective-permute-start | bytes 2451464 | tf_op jit(solution)/shard_map/ppermute | solution.py:263
  130.5 5.3 %collective-permute-start.19 = (bf16[336,1216]{1,0:T(8,128)(2,1)S(1)}, bf16[336,1216]{1,0:T(8,128)(2,1)}, u32[]{:S(2)}, u32[]{:S(2)}) collective-permute-start(bf16[336,1216]{1,0:T(8,128)(2,1)S(1)} %broadcast_select_fusion.refs_3_), channel_id=1, source_target_pairs={{0,4},{4,0},{1,5},{5,1},{2,6},{6,2},{3,7},{7,3},{8,12},{12,8},{9,1... | collective-permute-start | bytes 2451464 | tf_op jit(solution)/shard_map/ppermute | solution.py:263
  130.5 54.4 %collective-permute-start.25 = (bf16[512,896]{1,0:T(8,128)(2,1)S(1)}, bf16[512,896]{1,0:T(8,128)(2,1)}, u32[]{:S(2)}, u32[]{:S(2)}) collective-permute-start(bf16[512,896]{1,0:T(8,128)(2,1)S(1)} %copy-done.6), channel_id=1, source_target_pairs={{0,3},{1,2},{2,1},{3,0},{4,7},{5,6},{6,5},{7,4},{8,11},{9,10},{10,... | collective-permute-start | bytes 2752520 | tf_op jit(solution)/shard_map/ppermute | solution.py:266
  132.3 3.5 copy-start.12
  132.3 52.7 %collective-permute-start.24 = (bf16[512,896]{1,0:T(8,128)(2,1)}, bf16[512,896]{1,0:T(8,128)(2,1)}, u32[]{:S(2)}, u32[]{:S(2)}) collective-permute-start(bf16[512,896]{1,0:T(8,128)(2,1)} %get-tuple-element.111.refs_0_), channel_id=1, source_target_pairs={{0,3},{1,2},{2,1},{3,0},{4,7},{5,6},{6,5},{7,4},{8,11},{9,10},{10,... | collective-permute-start | bytes 2752520 | tf_op jit(solution)/shard_map/ppermute | solution.py:266
  182.6 23.5 %collective-permute-start.26 = (bf16[512,896]{1,0:T(8,128)(2,1)}, bf16[512,896]{1,0:T(8,128)(2,1)S(1)}, u32[]{:S(2)}, u32[]{:S(2)}) collective-permute-start(bf16[512,896]{1,0:T(8,128)(2,1)} %get-tuple-element.117), channel_id=1, source_target_pairs={{0,1},{1,0},{2,3},{3,2},{4,5},{5,4},{6,7},{7,6},{8,9},{9,8},{10,11... | collective-permute-start | bytes 2752520 | tf_op jit(solution)/shard_map/ppermute | solution.py:266
  183.4 42.2 %collective-permute-start.27 = (bf16[512,896]{1,0:T(8,128)(2,1)}, bf16[512,896]{1,0:T(8,128)(2,1)S(1)}, u32[]{:S(2)}, u32[]{:S(2)}) collective-permute-start(bf16[512,896]{1,0:T(8,128)(2,1)} %get-tuple-element.118), channel_id=1, source_target_pairs={{0,2},{1,3},{2,0},{3,1},{4,6},{5,7},{6,4},{7,5},{8,10},{9,11},{10,... | collective-permute-start | bytes 2752520 | tf_op jit(solution)/shard_map/ppermute | solution.py:266
  199.3 26.3 %collective-permute-start.28 = (bf16[512,896]{1,0:T(8,128)(2,1)}, bf16[512,896]{1,0:T(8,128)(2,1)S(1)}, u32[]{:S(2)}, u32[]{:S(2)}) collective-permute-start(bf16[512,896]{1,0:T(8,128)(2,1)} %get-tuple-element.119), channel_id=1, source_target_pairs={{0,3},{1,2},{2,1},{3,0},{4,7},{5,6},{6,5},{7,4},{8,11},{9,10},{10,... | collective-permute-start | bytes 2752520 | tf_op jit(solution)/shard_map/ppermute | solution.py:266
  206.1 19.6 %copy-start.7 = (bf16[512,896]{1,0:T(8,128)(2,1)}, bf16[512,896]{1,0:T(8,128)(2,1)S(1)}, u32[]{:S(2)}) copy-start(bf16[512,896]{1,0:T(8,128)(2,1)S(1)} %collective-permute-done.26.one) | copy-start | bytes 2752516
  252.3 32.5 %collective-permute-start.32 = (f32[256,512]{1,0:T(8,128)}, f32[256,512]{1,0:T(8,128)}, u32[]{:S(2)}, u32[]{:S(2)}) collective-permute-start(f32[256,512]{1,0:T(8,128)} %get-tuple-element.134), channel_id=1, source_target_pairs={{0,4},{4,0},{1,5},{5,1},{2,6},{6,2},{3,7},{7,3},{8,12},{12,8},{9,1... | collective-permute-start | bytes 1572872 | tf_op jit(solution)/shard_map/ppermute | solution.py:263
  284.8 37.4 %collective-permute-start.43 = (bf16[4,3,112,1216]{3,2,1,0:T(8,128)(2,1)}, bf16[4,3,112,1216]{3,2,1,0:T(8,128)(2,1)S(1)}, u32[]{:S(2)}, u32[]{:S(2)}) collective-permute-start(bf16[4,3,112,1216]{3,2,1,0:T(8,128)(2,1)} %get-tuple-element.149), channel_id=1, source_target_pairs={{0,4},{4,0},{1,5},{5,1},{2,6},{6,2},{3,7},{7,3},{8,12},{12,8},{9,1... | collective-permute-start | bytes 9805832 | tf_op jit(solution)/shard_map/ppermute | solution.py:263
  295.9 4.6 %collective-permute-start.33 = (bf16[4,128,2048]{2,1,0:T(8,128)(2,1)}, bf16[4,128,2048]{2,1,0:T(8,128)(2,1)}, u32[]{:S(2)}, u32[]{:S(2)}) collective-permute-start(bf16[4,128,2048]{2,1,0:T(8,128)(2,1)} %get-tuple-element.141), channel_id=1, source_target_pairs={{0,4},{4,0},{1,5},{5,1},{2,6},{6,2},{3,7},{7,3},{8,12},{12,8},{9,1... | collective-permute-start | bytes 6291464 | tf_op jit(solution)/shard_map/ppermute | solution.py:263
  296.4 24.5 %collective-permute-start.31 = (bf16[512,896]{1,0:T(8,128)(2,1)}, bf16[512,896]{1,0:T(8,128)(2,1)}, u32[]{:S(2)}, u32[]{:S(2)}) collective-permute-start(bf16[512,896]{1,0:T(8,128)(2,1)} %get-tuple-element.131), channel_id=1, source_target_pairs={{0,3},{1,2},{2,1},{3,0},{4,7},{5,6},{6,5},{7,4},{8,11},{9,10},{10,... | collective-permute-start | bytes 2752520 | tf_op jit(solution)/shard_map/ppermute | solution.py:266
  297.9 42.8 %collective-permute-start.30 = (bf16[512,896]{1,0:T(8,128)(2,1)}, bf16[512,896]{1,0:T(8,128)(2,1)}, u32[]{:S(2)}, u32[]{:S(2)}) collective-permute-start(bf16[512,896]{1,0:T(8,128)(2,1)} %get-tuple-element.130), channel_id=1, source_target_pairs={{0,2},{1,3},{2,0},{3,1},{4,6},{5,7},{6,4},{7,5},{8,10},{9,11},{10,... | collective-permute-start | bytes 2752520 | tf_op jit(solution)/shard_map/ppermute | solution.py:266
  299.3 43.3 %collective-permute-start.29 = (bf16[512,896]{1,0:T(8,128)(2,1)}, bf16[512,896]{1,0:T(8,128)(2,1)}, u32[]{:S(2)}, u32[]{:S(2)}) collective-permute-start(bf16[512,896]{1,0:T(8,128)(2,1)} %get-tuple-element.129), channel_id=1, source_target_pairs={{0,1},{1,0},{2,3},{3,2},{4,5},{5,4},{6,7},{7,6},{8,9},{9,8},{10,11... | collective-permute-start | bytes 2752520 | tf_op jit(solution)/shard_map/ppermute | solution.py:266
  305.1 46.8 %collective-permute-start.36 = (bf16[4,32,2048]{2,1,0:T(8,128)(2,1)}, bf16[4,32,2048]{2,1,0:T(8,128)(2,1)}, u32[]{:S(2)}, u32[]{:S(2)}) collective-permute-start(bf16[4,32,2048]{2,1,0:T(8,128)(2,1)} %get-tuple-element.145), channel_id=1, source_target_pairs={{0,3},{1,2},{2,1},{3,0},{4,7},{5,6},{6,5},{7,4},{8,11},{9,10},{10,... | collective-permute-start | bytes 1572872 | tf_op jit(solution)/shard_map/ppermute | solution.py:266
  320.9 41.1 %collective-permute-start.35 = (bf16[4,32,2048]{2,1,0:T(8,128)(2,1)}, bf16[4,32,2048]{2,1,0:T(8,128)(2,1)}, u32[]{:S(2)}, u32[]{:S(2)}) collective-permute-start(bf16[4,32,2048]{2,1,0:T(8,128)(2,1)} %get-tuple-element.144), channel_id=1, source_target_pairs={{0,2},{1,3},{2,0},{3,1},{4,6},{5,7},{6,4},{7,5},{8,10},{9,11},{10,... | collective-permute-start | bytes 1572872 | tf_op jit(solution)/shard_map/ppermute | solution.py:266
  322.1 39.9 %collective-permute-start.34 = (bf16[4,32,2048]{2,1,0:T(8,128)(2,1)}, bf16[4,32,2048]{2,1,0:T(8,128)(2,1)}, u32[]{:S(2)}, u32[]{:S(2)}) collective-permute-start(bf16[4,32,2048]{2,1,0:T(8,128)(2,1)} %get-tuple-element.143), channel_id=1, source_target_pairs={{0,1},{1,0},{2,3},{3,2},{4,5},{5,4},{6,7},{7,6},{8,9},{9,8},{10,11... | collective-permute-start | bytes 1572872 | tf_op jit(solution)/shard_map/ppermute | solution.py:266
  323.9 29.7 %copy-start = (f32[512,896]{1,0:T(8,128)S(1)}, f32[512,896]{1,0:T(8,128)}, u32[]{:S(2)}) copy-start(f32[512,896]{1,0:T(8,128)} %get-tuple-element.127.hidden) | copy-start | bytes 5505028
  323.9 29.7 %copy-start.10 = (bf16[512,896]{1,0:T(8,128)(2,1)S(1)}, bf16[512,896]{1,0:T(8,128)(2,1)}, u32[]{:S(2)}) copy-start(bf16[512,896]{1,0:T(8,128)(2,1)} %get-tuple-element.128) | copy-start | bytes 2752516
  340.6 25.4 %collective-permute-start.46 = (bf16[3,112,1216]{2,1,0:T(8,128)(2,1)}, bf16[3,112,1216]{2,1,0:T(8,128)(2,1)S(1)}, u32[]{:S(2)}, u32[]{:S(2)}) collective-permute-start(bf16[3,112,1216]{2,1,0:T(8,128)(2,1)} %get-tuple-element.153), channel_id=1, source_target_pairs={{0,8},{8,0},{16,24},{24,16},{1,9},{9,1},{17,25},{25,17},{2,10},{10... | collective-permute-start | bytes 2451464 | tf_op jit(solution)/shard_map/ppermute | solution.py:269
  342.7 39.9 %collective-permute-start.45 = (bf16[3,112,1216]{2,1,0:T(8,128)(2,1)}, bf16[3,112,1216]{2,1,0:T(8,128)(2,1)S(1)}, u32[]{:S(2)}, u32[]{:S(2)}) collective-permute-start(bf16[3,112,1216]{2,1,0:T(8,128)(2,1)} %get-tuple-element.152), channel_id=1, source_target_pairs={{0,24},{8,16},{16,8},{24,0},{1,25},{9,17},{17,9},{25,1},{2,26},{10... | collective-permute-start | bytes 2451464 | tf_op jit(solution)/shard_map/ppermute | solution.py:269
  351.9 10.2 %copy-start.5 = (f32[4,32,2048]{2,1,0:T(8,128)S(1)}, f32[4,32,2048]{2,1,0:T(8,128)}, u32[]{:S(2)}) copy-start(f32[4,32,2048]{2,1,0:T(8,128)} %get-tuple-element.142) | copy-start | bytes 3145732
  351.9 73.4 %collective-permute-start.44 = (bf16[3,112,1216]{2,1,0:T(8,128)(2,1)}, bf16[3,112,1216]{2,1,0:T(8,128)(2,1)S(1)}, u32[]{:S(2)}, u32[]{:S(2)}) collective-permute-start(bf16[3,112,1216]{2,1,0:T(8,128)(2,1)} %get-tuple-element.151), channel_id=1, source_target_pairs={{0,16},{8,24},{16,0},{24,8},{1,17},{9,25},{17,1},{25,9},{2,18},{10... | collective-permute-start | bytes 2451464 | tf_op jit(solution)/shard_map/ppermute | solution.py:269
  362.1 63.2 %copy-start.4 = (f32[3,112,1216]{2,1,0:T(8,128)S(1)}, f32[3,112,1216]{2,1,0:T(8,128)}, u32[]{:S(2)}) copy-start(f32[3,112,1216]{2,1,0:T(8,128)} %get-tuple-element.150) | copy-start | bytes 4902916
  363.9 61.7 %collective-permute-start.39 = (bf16[32,2048]{1,0:T(8,128)(2,1)S(1)}, bf16[32,2048]{1,0:T(8,128)(2,1)S(1)}, u32[]{:S(2)}, u32[]{:S(2)}) collective-permute-start(bf16[32,2048]{1,0:T(8,128)(2,1)S(1)} %get-tuple-element.160), channel_id=1, source_target_pairs={{0,8},{8,0},{16,24},{24,16},{1,9},{9,1},{17,25},{25,17},{2,10},{10... | collective-permute-start | bytes 393224 | tf_op jit(solution)/shard_map/ppermute | solution.py:269
  366.0 62.1 %collective-permute-start.38 = (bf16[32,2048]{1,0:T(8,128)(2,1)S(1)}, bf16[32,2048]{1,0:T(8,128)(2,1)S(1)}, u32[]{:S(2)}, u32[]{:S(2)}) collective-permute-start(bf16[32,2048]{1,0:T(8,128)(2,1)S(1)} %get-tuple-element.161), channel_id=1, source_target_pairs={{0,16},{8,24},{16,0},{24,8},{1,17},{9,25},{17,1},{25,9},{2,18},{10... | collective-permute-start | bytes 393224 | tf_op jit(solution)/shard_map/ppermute | solution.py:269
  366.0 62.1 %collective-permute-start.37 = (bf16[32,2048]{1,0:T(8,128)(2,1)S(1)}, bf16[32,2048]{1,0:T(8,128)(2,1)S(1)}, u32[]{:S(2)}, u32[]{:S(2)}) collective-permute-start(bf16[32,2048]{1,0:T(8,128)(2,1)S(1)} %get-tuple-element.159), channel_id=1, source_target_pairs={{0,24},{8,16},{16,8},{24,0},{1,25},{9,17},{17,9},{25,1},{2,26},{10... | collective-permute-start | bytes 393224 | tf_op jit(solution)/shard_map/ppermute | solution.py:269
  428.1 6.0 %collective-permute-start.40 = (bf16[32,2048]{1,0:T(8,128)(2,1)S(1)}, bf16[32,2048]{1,0:T(8,128)(2,1)S(1)}, u32[]{:S(2)}, u32[]{:S(2)}) collective-permute-start(bf16[32,2048]{1,0:T(8,128)(2,1)S(1)} %fusion.2), channel_id=1, source_target_pairs={{0,3},{1,2},{2,1},{3,0},{4,7},{5,6},{6,5},{7,4},{8,11},{9,10},{10,... | collective-permute-start | bytes 393224 | tf_op jit(solution)/shard_map/ppermute | solution.py:266
  429.6 5.8 %collective-permute-start.41 = (bf16[32,2048]{1,0:T(8,128)(2,1)S(1)}, bf16[32,2048]{1,0:T(8,128)(2,1)S(1)}, u32[]{:S(2)}, u32[]{:S(2)}) collective-permute-start(bf16[32,2048]{1,0:T(8,128)(2,1)S(1)} %fusion.2), channel_id=1, source_target_pairs={{0,2},{1,3},{2,0},{3,1},{4,6},{5,7},{6,4},{7,5},{8,10},{9,11},{10,... | collective-permute-start | bytes 393224 | tf_op jit(solution)/shard_map/ppermute | solution.py:266
  431.1 5.0 %collective-permute-start.42 = (bf16[32,2048]{1,0:T(8,128)(2,1)S(1)}, bf16[32,2048]{1,0:T(8,128)(2,1)S(1)}, u32[]{:S(2)}, u32[]{:S(2)}) collective-permute-start(bf16[32,2048]{1,0:T(8,128)(2,1)S(1)} %fusion.2), channel_id=1, source_target_pairs={{0,1},{1,0},{2,3},{3,2},{4,5},{5,4},{6,7},{7,6},{8,9},{9,8},{10,11... | collective-permute-start | bytes 393224 | tf_op jit(solution)/shard_map/ppermute | solution.py:266
  (4 other events, 5.7 us)
where the time goes:
time: 448 us; the launch traced here: 440 us
  waiting for transfers between devices  191 us (43%)
  Pallas kernels  160 us (36%)
  starting transfers between devices  66 us (15%)
  local copies, waits for them, and re-layouts  11.3 us (3%)
  other arithmetic  10.7 us (2%)
    ppermute x11, waiting for transfers between devices, ring(): lax.ppermute(value, 'shard', [(i, i ^ which) for i in range(self.shards)])  108 us
    ppermute x21, waiting for transfers between devices, side(): return lax.ppermute(value, 'tp', [(i, i ^ which) for i in range(self.tps)])  80.4 us
    pallas_call x3, Pallas kernels, mlp(): pl.pallas_call(functools.partial(mlp_body, chunks), grid=(chunks * steps,...  54.5 us
    ppermute x21, starting transfers between devices, side(): return lax.ppermute(value, 'tp', [(i, i ^ which) for i in range(self.tps)])  24.8 us
    ppermute x11, starting transfers between devices, ring(): lax.ppermute(value, 'shard', [(i, i ^ which) for i in range(self.shards)])  23.2 us
    pallas_call x1, Pallas kernels, weight_gradients(): pl.pallas_call(weight_gradients_body, grid=(3, 2), out_shape=(half, half)...  23 us
    pallas_call x1, Pallas kernels, attention_backward(): pl.pallas_call(attention_backward_body, out_shape=(jax.ShapeDtypeStruct((...  18.9 us
    ppermute x13, starting transfers between devices, across(): return lax.ppermute(value, 'ctx', pairs)  15.9 us
  transfers between devices with their start and end apart: 47, of which 21 were waited for; matrix products, arithmetic and copies ran while one was open for 3% of the time, Pallas kernels for 31%

commit v1 on v0

--- a/solution.py
+++ b/solution.py
@@ -27,10 +27,10 @@
     )
 
 
-def fill_bias(bias, doc_row, doc_col, row_start, row_count, span):
+def fill_bias(bias, doc_row, row_start, row_count, span):
     keys = lax.broadcasted_iota(jnp.int32, (span, row_count), 0)
     queries = lax.broadcasted_iota(jnp.int32, (span, row_count), 1) + row_start
-    key_doc = doc_col[0:span, :]
+    key_doc = jnp.broadcast_to(doc_row[:, 0:span], (8, span)).T[:, 0:1]
     query_doc = doc_row[:, row_start : row_start + row_count]
     same = (key_doc == query_doc) & (query_doc >= 0) & (keys <= queries)
     bias[0:span, :] = jnp.where(same | (keys == queries), 0.0, NEGATIVE)
@@ -58,7 +58,18 @@
 
 
 def attention_forward_body(
-    half_ref, doc_row, doc_col, query_t, own, other, mixed_t, lse, keys_t, keys, values_t, bias
+    half_ref,
+    doc_row,
+    query_t,
+    own,
+    other,
+    mixed_t,
+    exact_t,
+    lse,
+    keys_t,
+    keys,
+    values_t,
+    bias,
 ):
     token_count = query_t.shape[1]
     step = token_count // 2
@@ -71,7 +82,7 @@
                 span = half * token_count + (block + 1) * step
                 start = half * token_count + block * step
                 cols = slice(block * step, (block + 1) * step)
-                fill_bias(bias, doc_row, doc_col, start, step, span)
+                fill_bias(bias, doc_row, start, step, span)
 
                 def one(head):
                     group = lax.div(head, GROUP)
@@ -93,7 +104,9 @@
                         weight.astype(BF),
                         preferred_element_type=F32,
                     )
-                    mixed_t[place, cols] = (out / total).astype(BF)
+                    out = out / total
+                    exact_t[place, cols] = out
+                    mixed_t[place, cols] = out.astype(BF)
                     lse[head, :, cols] = jnp.broadcast_to(top + jnp.log(total), (8, step))
 
                 def several(index, carry):
@@ -104,7 +117,7 @@
                 lax.fori_loop(0, QUERY_HEADS // HEADS_PER_STEP, several, 0)
 
 
-def attention_forward(half, doc_row, doc_col, query_t, own, other):
+def attention_forward(half, doc_row, query_t, own, other):
     width, token_count = query_t.shape
     kv = KEY_VALUE_HEADS * HEAD_WIDTH
     vmem = pl.BlockSpec(memory_space=pltpu.VMEM)
@@ -112,10 +125,11 @@
         attention_forward_body,
         out_shape=(
             jax.ShapeDtypeStruct((width, token_count), BF),
+            jax.ShapeDtypeStruct((width, token_count), F32),
             jax.ShapeDtypeStruct((QUERY_HEADS, 8, token_count), F32),
         ),
-        in_specs=[pl.BlockSpec(memory_space=pltpu.SMEM)] + [vmem] * 5,
-        out_specs=(vmem, vmem),
+        in_specs=[pl.BlockSpec(memory_space=pltpu.SMEM)] + [vmem] * 4,
+        out_specs=(vmem, vmem, vmem),
         scratch_shapes=[
             pltpu.VMEM((kv, 2 * token_count), BF),
             pltpu.VMEM((KEY_VALUE_HEADS, 2 * token_count, HEAD_WIDTH), BF),
@@ -126,17 +140,17 @@
             flops=int(15e9), bytes_accessed=4 * width * token_count, transcendentals=0
         ),
         name="attention_forward",
-    )(half, doc_row, doc_col, query_t, own, other)
+    )(half, doc_row, query_t, own, other)
 
 
 def attention_backward_body(
     half_ref,
     doc_row,
-    doc_col,
     query_t,
     own,
     other,
     grad_t,
+    exact_t,
     lse,
     grad_query_t,
     own_sums,
@@ -162,7 +176,7 @@
                 span = half * token_count + (block + 1) * step
                 start = half * token_count + block * step
                 cols = slice(block * step, (block + 1) * step)
-                fill_bias(bias, doc_row, doc_col, start, step, span)
+                fill_bias(bias, doc_row, start, step, span)
 
                 def one(head):
                     group = lax.div(head, GROUP)
@@ -176,7 +190,7 @@
                     )
                     prob = jnp.exp(score - lse[head, 0:1, cols])
                     grad_prob = jnp.dot(values[group, 0:span, :], grad, preferred_element_type=F32)
-                    delta = jnp.sum(prob * grad_prob, axis=0, keepdims=True)
+                    delta = jnp.sum(grad.astype(F32) * exact_t[place, cols], axis=0, keepdims=True)
                     grad_score = (prob * (grad_prob - delta)).astype(BF)
                     grad_value[group, 0:span, :] += dot(prob.astype(BF), grad, 1, 1)
                     grad_key[group, 0:span, :] += dot(grad_score, query, 1, 1)
@@ -204,7 +218,7 @@
                     other_sums[rows, :] = first
 
 
-def attention_backward(half, doc_row, doc_col, query_t, own, other, grad_t, lse):
+def attention_backward(half, doc_row, query_t, own, other, grad_t, exact_t, lse):
     width, token_count = query_t.shape
     kv = KEY_VALUE_HEADS * HEAD_WIDTH
     vmem = pl.BlockSpec(memory_space=pltpu.VMEM)
@@ -228,7 +242,7 @@
             flops=int(35e9), bytes_accessed=8 * width * token_count, transcendentals=0
         ),
         name="attention_backward",
-    )(half, doc_row, doc_col, query_t, own, other, grad_t, lse)
+    )(half, doc_row, query_t, own, other, grad_t, exact_t, lse)
 
 
 def rope_tables(half, token_count):
@@ -286,7 +300,8 @@
         theirs = [self.across(piece) for piece in mine]
         return far, sides, mine, theirs
 
-    def gather_line(self, block, later):
+    def gather_line(self, block, after, later):
+        block, after = lax.optimization_barrier((block, after))
         two = self.ring(block, 2)
         one = self.ring(block, 1)
         late, relayed, later = lax.optimization_barrier((block, two, later))
@@ -347,10 +362,12 @@
         return parts[:1] + [self.side(parts[which], which) for which in (1, 2, 3)]
 
     def scatter_line(self, send, keep):
-        pieces = fold_line(self.place(), keep, self.across(send))
-        total = pieces[0]
+        received = self.across(send)
+        part = (keep.astype(F32) + received.astype(F32)).astype(BF)
+        total = lax.dynamic_index_in_dim(part, self.z, 0, False).astype(F32)
         for which in (2, 3, 1):
-            total = total + self.ring(pieces[which], which).astype(F32)
+            piece = lax.dynamic_index_in_dim(part, self.z ^ which, 0, False)
+            total = total + self.ring(piece, which).astype(F32)
         return total
 
 
@@ -536,32 +553,6 @@
             flops=0, bytes_accessed=6 * blocks * rows * cols, transcendentals=0
         ),
         name="fold",
-    )(place, keep, received)
-
-
-def fold_line_body(place, keep, received, *outs):
-    for which, out in enumerate(outs):
-
-        @pl.when(pl.program_id(0) == which)
-        def _():
-            value = keep[0].astype(F32) + received[0].astype(F32)
-            out[...] = value.astype(out.dtype)
-
-
-def fold_line(place, keep, received):
-    shape = keep.shape[1:]
-    block = pl.BlockSpec((1,) + shape, lambda i, place: (i ^ place[0], 0, 0, 0))
-    out = pl.BlockSpec(shape, lambda i, place: (0, 0, 0))
-    return pl.pallas_call(
-        fold_line_body,
-        out_shape=(jax.ShapeDtypeStruct(shape, F32),) + (jax.ShapeDtypeStruct(shape, BF),) * 3,
-        grid_spec=pltpu.PrefetchScalarGridSpec(
-            num_scalar_prefetch=1, grid=(4,), in_specs=[block] * 2, out_specs=(out,) * 4
-        ),
-        cost_estimate=pl.CostEstimate(
-            flops=0, bytes_accessed=6 * keep.size, transcendentals=0
-        ),
-        name="fold_line",
     )(place, keep, received)
 
 
@@ -885,12 +876,12 @@
         0,
     )
     if mesh.fast:
-        _, sides, mine, theirs = mesh.gather_spread(packed)
+        far, sides, mine, theirs = mesh.gather_spread(packed)
         cosine, sine = rope_tables(mesh.c, token_count)
         fused_weight, output_weight, query_t, own, first_gain, second_gain = project(
             mesh.place(), mine, theirs, tokens, cosine, sine, fused_width
         )
-        line = mesh.gather_line(jnp.concatenate([w_gate, w_up, w_down.T], 0), own)
+        line = mesh.gather_line(jnp.concatenate([w_gate, w_up, w_down.T], 0), far, own)
         others = [mesh.across(part) for part in line]
         late, sides = lax.optimization_barrier((cotangent, sides))
         grad_parts = mesh.gather_tokens(late)
@@ -923,8 +914,7 @@
         first_gain, second_gain = first_gain[None], second_gain[None]
     other = mesh.across(own)
     half = mesh.c.astype(jnp.int32).reshape(1)
-    doc_col = doc_ids.reshape(-1, 1)
-    mixed_t, lse = attention_forward(half, doc_ids, doc_col, query_t, own, other)
+    mixed_t, exact_t, lse = attention_forward(half, doc_ids, query_t, own, other)
 
     hidden, normed_mlp = output_projection(tokens, mixed_t, output_weight, second_gain)
     normed_parts = mesh.gather_tokens(normed_mlp)
@@ -971,7 +961,7 @@
         back_parts, hidden, cotangent, output_weight, second_gain
     )
     grad_query_rot, own_sums, to_other = attention_backward(
-        half, doc_ids, doc_col, query_t, own, other, grad_mixed_t, lse
+        half, doc_ids, query_t, own, other, grad_mixed_t, exact_t, lse
     )
     hidden_late, grad_query_rot = lax.optimization_barrier((hidden, grad_query_rot))
     result = (hidden_late + mesh.scatter_tokens(downs).astype(F32)).astype(BF)

time: 448 us -> 423 us (0.944)
  waiting for transfers between devices: 191 us -> 175 us
  Pallas kernels: 160 us -> 151 us
    ppermute x21, waiting for transfers between devices: 80.4 us -> 59.8 us  [side(): return lax.ppermute(value, 'tp', [(i, i ^ which) for i in range(self.tps)])]
    pallas_call x1 -> x0, Pallas kernels: 6.76 us -> none  [fold_line(): pl.pallas_call(fold_line_body, out_shape=(jax.ShapeDtypeStruct(shape, F32...]
  transfers between devices with their start and end apart: 47 -> 47, of which waited for: 21 -> 21; matrix products, arithmetic and copies ran while one was open for 3% -> 3% of each run, Pallas kernels for 31% -> 36%
where the time goes in v1:
time: 423 us; the launch traced here: 415 us
  waiting for transfers between devices  175 us (41%)
  Pallas kernels  151 us (36%)
  starting transfers between devices  65 us (15%)
  other arithmetic  12.3 us (3%)
  local copies, waits for them, and re-layouts  11 us (3%)
    ppermute x11, waiting for transfers between devices, ring(): lax.ppermute(value, 'shard', [(i, i ^ which) for i in range(self.shards)])  110 us
    ppermute x21, waiting for transfers between devices, side(): return lax.ppermute(value, 'tp', [(i, i ^ which) for i in range(self.tps)])  59.8 us
    pallas_call x3, Pallas kernels, mlp(): pl.pallas_call(functools.partial(mlp_body, chunks), grid=(chunks * steps,...  54.6 us
    ppermute x21, starting transfers between devices, side(): return lax.ppermute(value, 'tp', [(i, i ^ which) for i in range(self.tps)])  25.7 us
    ppermute x11, starting transfers between devices, ring(): lax.ppermute(value, 'shard', [(i, i ^ which) for i in range(self.shards)])  23.2 us
    pallas_call x1, Pallas kernels, weight_gradients(): pl.pallas_call(weight_gradients_body, grid=(3, 2), out_shape=(half, half)...  22.8 us
    pallas_call x1, Pallas kernels, attention_forward(): pl.pallas_call(attention_forward_body, out_shape=(jax.ShapeDtypeStruct((w...  16.2 us
    pallas_call x1, Pallas kernels, attention_backward(): pl.pallas_call(attention_backward_body, out_shape=(jax.ShapeDtypeStruct((...  16.1 us
  transfers between devices with their start and end apart: 47, of which 21 were waited for; matrix products, arithmetic and copies ran while one was open for 3% of the time, Pallas kernels for 36%

profile of v1, /device:TPU:0, one launch (start us, length us, event | category | flops | bytes accessed | tf_op | source)
XLA Modules:
  0.0 415.0 jit_solution(10884618788313371747)
XLA Ops:
  4.1 1.1 pad_maximum_fusion.1
  5.7 3.1 collective-permute-start
  8.8 2.6 collective-permute-start.1
  11.4 2.5 collective-permute-done
  13.9 7.8 %collective-permute-done.1 = bf16[32,2048]{1,0:T(8,128)(2,1)S(1)} collective-permute-done((bf16[32,2048]{1,0:T(8,128)(2,1)S(1)}, bf16[32,2048]{1,0:T(8,128)(2,1)S(1)}, u32[]{:S(2)}, u32[]{:S(2)}) %collective-permute-start.1) | collective-permute-done | bytes 131104 | tf_op jit(solution)/shard_map/ppermute | solution.py:283
  21.7 1.6 collective-permute-start.3
  23.3 1.5 collective-permute-start.4
  25.5 8.3 %collective-permute-done.3.refs_2_ = bf16[96,2048]{1,0:T(8,128)(2,1)S(1)} collective-permute-done((bf16[96,2048]{1,0:T(8,128)(2,1)S(1)}, bf16[96,2048]{1,0:T(8,128)(2,1)S(1)}, u32[]{:S(2)}, u32[]{:S(2)}) %collective-permute-start.3) | collective-permute-done | bytes 393248 | tf_op jit(solution)/shard_map/ppermute | solution.py:280
  33.8 6.1 %collective-permute-done.4.refs_3_ = bf16[96,2048]{1,0:T(8,128)(2,1)S(1)} collective-permute-done((bf16[96,2048]{1,0:T(8,128)(2,1)S(1)}, bf16[96,2048]{1,0:T(8,128)(2,1)S(1)}, u32[]{:S(2)}, u32[]{:S(2)}) %collective-permute-start.4) | collective-permute-done | bytes 393248 | tf_op jit(solution)/shard_map/ppermute | solution.py:280
  40.4 4.6 %collective-permute-start.13 = (bf16[336,1216]{1,0:T(8,128)(2,1)S(1)}, bf16[336,1216]{1,0:T(8,128)(2,1)S(1)}, u32[]{:S(2)}, u32[]{:S(2)}) collective-permute-start(bf16[336,1216]{1,0:T(8,128)(2,1)S(1)} %pad_maximum_fusion.refs_0_), channel_id=1, source_target_pairs={{0,16},{8,24},{16,0},{24,8},{1,17},{9,25},{17,1},{25,9},{2,18},{10... | collective-permute-start | bytes 2451464 | tf_op jit(solution)/shard_map/ppermute | solution.py:283
  46.6 7.3 %project.1 = (bf16[896,1152]{1,0:T(8,128)(2,1)}, bf16[896,896]{1,0:T(8,128)(2,1)}, bf16[896,512]{1,0:T(8,128)(2,1)}, bf16[256,512]{1,0:T(8,128)(2,1)}, f32[1,896]{1,0:T(1,128)}, /*index=5*/f32[1,896]{1,0:T(1,128)}) custom-call(s32[3]{0:T(128)} %pad_add_fusion.place, bf16[128,2048]{1,0:T(8,128)(2,1)} %copy-done.13, bf16[96,2048]{1,0:T(8,128)(2,1)} %copy-done.17, ...), custom_call_target="tpu_custom_call" | custom-call | flops 3000000000 | bytes 12000000 | tf_op jit(solution)/shard_map/project/pallas_call | solution.py:452
  53.9 1.0 collective-permute-start.22
  55.0 1.1 collective-permute-start.23
  56.1 26.7 %collective-permute-done.13.refs_2_ = bf16[336,1216]{1,0:T(8,128)(2,1)S(1)} collective-permute-done((bf16[336,1216]{1,0:T(8,128)(2,1)S(1)}, bf16[336,1216]{1,0:T(8,128)(2,1)S(1)}, u32[]{:S(2)}, u32[]{:S(2)}) %collective-permute-start.13) | collective-permute-done | bytes 817184 | tf_op jit(solution)/shard_map/ppermute | solution.py:283
  83.5 1.3 collective-permute-start.15
  84.8 16.2 %attention_forward.1 = (bf16[896,512]{1,0:T(8,128)(2,1)}, f32[896,512]{1,0:T(8,128)}, f32[14,8,512]{2,1,0:T(8,128)}) custom-call(s32[1]{0:T(128)} %bitcast.half_ref, s32[1,1024]{1,0:T(1,128)} %doc_row.3, bf16[896,512]{1,0:T(8,128)(2,1)} %get-tuple-element.82.query_t, bf16[256,512]{1,0:T(8,128)(2,1)} %get-tuple-element.83.own, ...), custom_call_target="tpu_custom_call" | custom-call | flops 15000000512 | bytes 1835008 | tf_op jit(solution)/shard_map/attention_forward/pallas_call | solution.py:124
  101.0 4.9 %output_projection.1 = (f32[512,896]{1,0:T(8,128)}, bf16[512,896]{1,0:T(8,128)(2,1)}) custom-call(bf16[512,896]{1,0:T(8,128)(2,1)} %tokens.3, bf16[896,512]{1,0:T(8,128)(2,1)} %get-tuple-element.84.mixed_t, bf16[896,896]{1,0:T(8,128)(2,1)} %get-tuple-element.85.weight, f32[1,896]{1,0:T(1,128)} %get-tuple-element.86.gain), custom_call_target="tpu_custom_call" | custom-call | flops 1000000000 | bytes 6000000 | tf_op jit(solution)/shard_map/output_projection/pallas_call | solution.py:485
  105.8 1.3 collective-permute-start.20
  107.1 3.5 collective-permute-start.12
  111.4 1.2 broadcast_select_fusion.refs_3_
  112.7 12.8 %collective-permute-done.12.refs_1_ = bf16[336,1216]{1,0:T(8,128)(2,1)} collective-permute-done((bf16[336,1216]{1,0:T(8,128)(2,1)S(1)}, bf16[336,1216]{1,0:T(8,128)(2,1)}, u32[]{:S(2)}, u32[]{:S(2)}) %collective-permute-start.12) | collective-permute-done | bytes 817184 | tf_op jit(solution)/shard_map/ppermute | solution.py:283
  125.5 5.0 %collective-permute-start.16 = (bf16[336,1216]{1,0:T(8,128)(2,1)S(1)}, bf16[336,1216]{1,0:T(8,128)(2,1)S(1)}, u32[]{:S(2)}, u32[]{:S(2)}) collective-permute-start(bf16[336,1216]{1,0:T(8,128)(2,1)S(1)} %pad_maximum_fusion.refs_0_), channel_id=1, source_target_pairs={{0,4},{4,0},{1,5},{5,1},{2,6},{6,2},{3,7},{7,3},{8,12},{12,8},{9,1... | collective-permute-start | bytes 2451464 | tf_op jit(solution)/shard_map/ppermute | solution.py:277
  131.1 1.7 collective-permute-start.25
  132.8 1.4 collective-permute-start.24
  135.2 1.2 collective-permute-done.19.refs_7_
  136.4 6.7 %assemble_line.1.refs_2_.refs_3_.refs_4_.refs_5_.refs_6_ = bf16[3,896,1216]{2,1,0:T(8,128)(2,1)} custom-call(s32[3]{0:T(128)} %pad_add_fusion.place, bf16[336,1216]{1,0:T(8,128)(2,1)} %copy-done.2, bf16[336,1216]{1,0:T(8,128)(2,1)} %collective-permute-done.12.refs_1_, bf16[336,1216]{1,0:T(8,128)(2,1)} %copy-done.11, bf16[336,1216]{1,0:T(8,128)(2,1)} %copy-done.3, ...), custom_call_target="tpu_custom_call" | custom-call | bytes 13074432 | tf_op jit(solution)/shard_map/assemble_line/pallas_call | solution.py:579
  143.1 14.3 %mlp.3 = (bf16[512,896]{1,0:T(8,128)(2,1)}, bf16[512,896]{1,0:T(8,128)(2,1)}, bf16[3,2048,1216]{2,1,0:T(8,128)(2,1)}, bf16[2,896,2048]{2,1,0:T(8,128)(2,1)}) custom-call(bf16[512,896]{1,0:T(8,128)(2,1)} %get-tuple-element.110.refs_0_, bf16[512,896]{1,0:T(8,128)(2,1)} %cotangent.1, bf16[3,896,1216]{2,1,0:T(8,128)(2,1)} %assemble_line.1.refs_2_.refs_3_.refs_4_.refs_5_.refs_6_, ...), custom_call_target="tpu_custom_call" | custom-call | flops 6694109184 | bytes 15187968 | tf_op jit(solution)/shard_map/mlp/pallas_call | solution.py:759
  157.4 25.9 %mlp.4 = (bf16[512,896]{1,0:T(8,128)(2,1)}, bf16[512,896]{1,0:T(8,128)(2,1)}, bf16[512,896]{1,0:T(8,128)(2,1)}, bf16[512,896]{1,0:T(8,128)(2,1)}, bf16[3,2048,12...) custom-call(bf16[512,896]{1,0:T(8,128)(2,1)} %collective-permute-done.20.refs_0_, ...), custom_call_target="tpu_custom_call", output_to_operand_aliasing={{4}: (7, {}), {5}: (8, {})} | custom-call | flops 13388218368 | bytes 23838720 | tf_op jit(solution)/shard_map/mlp/pallas_call | solution.py:759
  184.0 1.5 collective-permute-start.27
  185.6 14.5 %mlp.5 = (bf16[512,896]{1,0:T(8,128)(2,1)}, bf16[512,896]{1,0:T(8,128)(2,1)}, bf16[3,2048,1216]{2,1,0:T(8,128)(2,1)}, bf16[2,896,2048]{2,1,0:T(8,128)(2,1)}) custom-call(bf16[512,896]{1,0:T(8,128)(2,1)} %collective-permute-done.24.refs_0_, bf16[512,896]{1,0:T(8,128)(2,1)} %collective-permute-done.25.refs_1_, ...), custom_call_target="tpu_custom_call", output_to_operand_aliasing={{2}: (5, {}), {3}: (6, {})} | custom-call | flops 6694109184 | bytes 15187968 | tf_op jit(solution)/shard_map/mlp/pallas_call | solution.py:759
  200.1 1.3 collective-permute-start.28
  201.3 22.8 %weight_gradients.1 = (bf16[4,3,112,1216]{3,2,1,0:T(8,128)(2,1)}, bf16[4,3,112,1216]{3,2,1,0:T(8,128)(2,1)}) custom-call(s32[3]{0:T(128)} %pad_add_fusion.place, bf16[2,896,2048]{2,1,0:T(8,128)(2,1)} %get-tuple-element.146.left, bf16[3,2048,1216]{2,1,0:T(8,128)(2,1)} %get-tuple-element.147.right), custom_call_target="tpu_custom_call" | custom-call | flops 13388218368 | bytes 25952256 | tf_op jit(solution)/shard_map/weight_gradients/pallas_call | solution.py:819
  224.1 2.2 collective-permute-done.27.two
  227.5 6.5 %middle.1 = (f32[512,896]{1,0:T(8,128)}, bf16[896,512]{1,0:T(8,128)(2,1)}, f32[1,896]{1,0:T(1,128)}) custom-call(bf16[512,896]{1,0:T(8,128)(2,1)} %get-tuple-element.119.own, bf16[512,896]{1,0:T(8,128)(2,1)} %copy-done.7, bf16[512,896]{1,0:T(8,128)(2,1)} %copy-done.8, bf16[512,896]{1,0:T(8,128)(2,1)} %copy-done.9, f32[512,896]{1,0:T(8,128)} %get-tuple-element.127.hidden, ...), custom_call_target="tpu_custom_call" | custom-call | flops 1000000000 | bytes 9000000 | tf_op jit(solution)/shard_map/middle/pallas_call | solution.py:517
  234.0 16.1 %attention_backward.1 = (bf16[896,512]{1,0:T(8,128)(2,1)}, f32[256,512]{1,0:T(8,128)}, f32[256,512]{1,0:T(8,128)}) custom-call(s32[1]{0:T(128)} %bitcast.half_ref, s32[1,1024]{1,0:T(1,128)} %doc_row.3, bf16[896,512]{1,0:T(8,128)(2,1)} %get-tuple-element.82.query_t, bf16[256,512]{1,0:T(8,128)(2,1)} %get-tuple-element.83.own, ...), custom_call_target="tpu_custom_call" | custom-call | flops 35000000512 | bytes 3670016 | tf_op jit(solution)/shard_map/attention_backward/pallas_call | solution.py:227
  250.2 7.6 %collective-permute-start.32 = (f32[256,512]{1,0:T(8,128)}, f32[256,512]{1,0:T(8,128)S(1)}, u32[]{:S(2)}, u32[]{:S(2)}) collective-permute-start(f32[256,512]{1,0:T(8,128)} %get-tuple-element.134), channel_id=1, source_target_pairs={{0,4},{4,0},{1,5},{5,1},{2,6},{6,2},{3,7},{7,3},{8,12},{12,8},{9,1... | collective-permute-start | bytes 1572872 | tf_op jit(solution)/shard_map/ppermute | solution.py:277
  257.7 1.7 collective-permute-done.32.other_sums
  260.3 11.2 %projection_gradients.1 = (bf16[512,896]{1,0:T(8,128)(2,1)}, bf16[4,128,2048]{2,1,0:T(8,128)(2,1)}, bf16[4,128,2048]{2,1,0:T(8,128)(2,1)}) custom-call(s32[3]{0:T(128)} %pad_add_fusion.place, bf16[896,512]{1,0:T(8,128)(2,1)} %get-tuple-element.132.grad_query, f32[256,512]{1,0:T(8,128)} %get-tuple-element.133.own_sums, f32[256,512]{1,0:T(8,128)} %copy-done.21, ...), custom_call_target="tpu_custom_call" | custom-call | flops 6000000000 | bytes 16000000 | tf_op jit(solution)/shard_map/projection_gradients/pallas_call | solution.py:683
  271.9 1.4 collective-permute-start.31
  273.2 1.5 collective-permute-start.30
  275.9 1.4 copy-done.4
  277.3 4.6 %fold.1 = (f32[4,32,2048]{2,1,0:T(8,128)}, bf16[4,32,2048]{2,1,0:T(8,128)(2,1)}, bf16[4,32,2048]{2,1,0:T(8,128)(2,1)}, bf16[4,32,2048]{2,1,0:T(8,128)(2,1)}) custom-call(s32[3]{0:T(128)} %pad_add_fusion.place, bf16[4,128,2048]{2,1,0:T(8,128)(2,1)} %get-tuple-element.140.keep, bf16[4,128,2048]{2,1,0:T(8,128)(2,1)} %copy-done.4), custom_call_target="tpu_custom_call" | custom-call | bytes 6291456 | tf_op jit(solution)/shard_map/fold/pallas_call | solution.py:545
  281.8 1.4 collective-permute-start.36
  283.2 2.9 add_convert_fusion
  286.1 1.6 collective-permute-start.35
  287.7 8.7 %collective-permute-done.31 = bf16[512,896]{1,0:T(8,128)(2,1)} collective-permute-done((bf16[512,896]{1,0:T(8,128)(2,1)}, bf16[512,896]{1,0:T(8,128)(2,1)}, u32[]{:S(2)}, u32[]{:S(2)}) %collective-permute-start.31) | collective-permute-done | bytes 917536 | tf_op jit(solution)/shard_map/ppermute | solution.py:280
  296.4 1.4 collective-permute-start.34
  298.0 18.1 %collective-permute-done.30 = bf16[512,896]{1,0:T(8,128)(2,1)} collective-permute-done((bf16[512,896]{1,0:T(8,128)(2,1)}, bf16[512,896]{1,0:T(8,128)(2,1)}, u32[]{:S(2)}, u32[]{:S(2)}) %collective-permute-start.30) | collective-permute-done | bytes 917536 | tf_op jit(solution)/shard_map/ppermute | solution.py:280
  316.1 2.0 collective-permute-start.46
  318.1 1.1 collective-permute-start.45
  319.2 8.0 %collective-permute-done.36 = bf16[4,32,2048]{2,1,0:T(8,128)(2,1)S(1)} collective-permute-done((bf16[4,32,2048]{2,1,0:T(8,128)(2,1)}, bf16[4,32,2048]{2,1,0:T(8,128)(2,1)S(1)}, u32[]{:S(2)}, u32[]{:S(2)}) %collective-permute-start.36) | collective-permute-done | bytes 524320 | tf_op jit(solution)/shard_map/ppermute | solution.py:280
  327.2 1.7 collective-permute-start.44
  328.9 3.3 add_convert_fusion.1
  332.1 5.4 %collective-permute-done.35 = bf16[4,32,2048]{2,1,0:T(8,128)(2,1)S(1)} collective-permute-done((bf16[4,32,2048]{2,1,0:T(8,128)(2,1)S(1)}, bf16[4,32,2048]{2,1,0:T(8,128)(2,1)S(1)}, u32[]{:S(2)}, u32[]{:S(2)}) %collective-permute-start.35) | collective-permute-done | bytes 524320 | tf_op jit(solution)/shard_map/ppermute | solution.py:280
  337.8 2.1 collective-permute-start.39
  339.9 2.4 collective-permute-start.37
  342.4 15.4 %collective-permute-done.45 = bf16[3,112,1216]{2,1,0:T(8,128)(2,1)S(1)} collective-permute-done((bf16[3,112,1216]{2,1,0:T(8,128)(2,1)S(1)}, bf16[3,112,1216]{2,1,0:T(8,128)(2,1)S(1)}, u32[]{:S(2)}, u32[]{:S(2)}) %collective-permute-start.45) | collective-permute-done | bytes 817184 | tf_op jit(solution)/shard_map/ppermute | solution.py:283
  357.7 42.7 %collective-permute-done.44 = bf16[3,112,1216]{2,1,0:T(8,128)(2,1)S(1)} collective-permute-done((bf16[3,112,1216]{2,1,0:T(8,128)(2,1)S(1)}, bf16[3,112,1216]{2,1,0:T(8,128)(2,1)S(1)}, u32[]{:S(2)}, u32[]{:S(2)}) %collective-permute-start.44) | collective-permute-done | bytes 817184 | tf_op jit(solution)/shard_map/ppermute | solution.py:283
  400.9 2.4 collective-permute-done.38
  403.3 1.4 collective-permute-start.40
  404.8 1.5 collective-permute-start.41
  406.9 1.2 slice_bitcast_fusion
  408.1 1.3 collective-permute-done.40
  409.4 1.3 collective-permute-done.41
  (124 shorter events, 19.8 us)
Async XLA Ops:
  0.6 24.6 %copy-start.14 = (bf16[1216,112]{0,1:T(8,128)(2,1)S(1)}, bf16[1216,112]{0,1:T(8,128)(2,1)}, u32[]{:S(2)}) copy-start(bf16[1216,112]{0,1:T(8,128)(2,1)} %param.28) | copy-start | bytes 817156
  0.7 24.6 %copy-start.15 = (bf16[112,1216]{1,0:T(8,128)(2,1)S(1)}, bf16[112,1216]{1,0:T(8,128)(2,1)}, u32[]{:S(2)}) copy-start(bf16[112,1216]{1,0:T(8,128)(2,1)} %param.27) | copy-start | bytes 817156
  0.7 24.6 %copy-start.16 = (bf16[112,1216]{1,0:T(8,128)(2,1)S(1)}, bf16[112,1216]{1,0:T(8,128)(2,1)}, u32[]{:S(2)}) copy-start(bf16[112,1216]{1,0:T(8,128)(2,1)} %param.26) | copy-start | bytes 817156
  5.6 40.9 %copy-start.13 = (bf16[128,2048]{1,0:T(8,128)(2,1)}, bf16[128,2048]{1,0:T(8,128)(2,1)S(1)}, u32[]{:S(2)}) copy-start(bf16[128,2048]{1,0:T(8,128)(2,1)S(1)} %concatenate.16.refs_0_) | copy-start | bytes 1572868
  5.7 8.2 %collective-permute-start = (bf16[32,2048]{1,0:T(8,128)(2,1)S(1)}, bf16[32,2048]{1,0:T(8,128)(2,1)S(1)}, u32[]{:S(2)}, u32[]{:S(2)}) collective-permute-start(bf16[32,2048]{1,0:T(8,128)(2,1)S(1)} %constant_dynamic-slice_fusion.4), channel_id=1, source_target_pairs={{0,8},{8,0},{16,24},{24,16},{1,9},{9,1},{17,25},{25,17},{2,10},{10... | collective-permute-start | bytes 393224 | tf_op jit(solution)/shard_map/ppermute | solution.py:283
  8.8 12.9 %collective-permute-start.1 = (bf16[32,2048]{1,0:T(8,128)(2,1)S(1)}, bf16[32,2048]{1,0:T(8,128)(2,1)S(1)}, u32[]{:S(2)}, u32[]{:S(2)}) collective-permute-start(bf16[32,2048]{1,0:T(8,128)(2,1)S(1)} %constant_dynamic-slice_fusion.4), channel_id=1, source_target_pairs={{0,16},{8,24},{16,0},{24,8},{1,17},{9,25},{17,1},{25,9},{2,18},{10... | collective-permute-start | bytes 393224 | tf_op jit(solution)/shard_map/ppermute | solution.py:283
  11.4 10.3 %collective-permute-start.2 = (bf16[32,2048]{1,0:T(8,128)(2,1)S(1)}, bf16[32,2048]{1,0:T(8,128)(2,1)S(1)}, u32[]{:S(2)}, u32[]{:S(2)}) collective-permute-start(bf16[32,2048]{1,0:T(8,128)(2,1)S(1)} %constant_dynamic-slice_fusion.4), channel_id=1, source_target_pairs={{0,24},{8,16},{16,8},{24,0},{1,25},{9,17},{17,9},{25,1},{2,26},{10... | collective-permute-start | bytes 393224 | tf_op jit(solution)/shard_map/ppermute | solution.py:283
  11.4 29.0 %collective-permute-start.6 = (bf16[128,2048]{1,0:T(8,128)(2,1)S(1)}, bf16[128,2048]{1,0:T(8,128)(2,1)}, u32[]{:S(2)}, u32[]{:S(2)}) collective-permute-start(bf16[128,2048]{1,0:T(8,128)(2,1)S(1)} %concatenate.16.refs_0_), channel_id=1, source_target_pairs={{0,4},{4,0},{1,5},{5,1},{2,6},{6,2},{3,7},{7,3},{8,12},{12,8},{9,1... | collective-permute-start | bytes 1572872 | tf_op jit(solution)/shard_map/ppermute | solution.py:277
  21.7 24.9 %copy-start.17 = (bf16[96,2048]{1,0:T(8,128)(2,1)}, bf16[96,2048]{1,0:T(8,128)(2,1)S(1)}, u32[]{:S(2)}) copy-start(bf16[96,2048]{1,0:T(8,128)(2,1)S(1)} %constant_dynamic-update-slice_fusion.refs_1_) | copy-start | bytes 1179652
  21.7 12.1 %collective-permute-start.3 = (bf16[96,2048]{1,0:T(8,128)(2,1)S(1)}, bf16[96,2048]{1,0:T(8,128)(2,1)S(1)}, u32[]{:S(2)}, u32[]{:S(2)}) collective-permute-start(bf16[96,2048]{1,0:T(8,128)(2,1)S(1)} %constant_dynamic-update-slice_fusion.refs_1_), channel_id=1, source_target_pairs={{0,1},{1,0},{2,3},{3,2},{4,5},{5,4},{6,7},{7,6},{8,9},{9,8},{10,11... | collective-permute-start | bytes 1179656 | tf_op jit(solution)/shard_map/ppermute | solution.py:280
  23.3 16.6 %collective-permute-start.4 = (bf16[96,2048]{1,0:T(8,128)(2,1)S(1)}, bf16[96,2048]{1,0:T(8,128)(2,1)S(1)}, u32[]{:S(2)}, u32[]{:S(2)}) collective-permute-start(bf16[96,2048]{1,0:T(8,128)(2,1)S(1)} %constant_dynamic-update-slice_fusion.refs_1_), channel_id=1, source_target_pairs={{0,2},{1,3},{2,0},{3,1},{4,6},{5,7},{6,4},{7,5},{8,10},{9,11},{10,... | collective-permute-start | bytes 1179656 | tf_op jit(solution)/shard_map/ppermute | solution.py:280
  24.8 15.1 %collective-permute-start.5 = (bf16[96,2048]{1,0:T(8,128)(2,1)S(1)}, bf16[96,2048]{1,0:T(8,128)(2,1)}, u32[]{:S(2)}, u32[]{:S(2)}) collective-permute-start(bf16[96,2048]{1,0:T(8,128)(2,1)S(1)} %constant_dynamic-update-slice_fusion.refs_1_), channel_id=1, source_target_pairs={{0,3},{1,2},{2,1},{3,0},{4,7},{5,6},{6,5},{7,4},{8,11},{9,10},{10,... | collective-permute-start | bytes 1179656 | tf_op jit(solution)/shard_map/ppermute | solution.py:280
  25.4 100.2 %copy-start.2 = (bf16[336,1216]{1,0:T(8,128)(2,1)}, bf16[336,1216]{1,0:T(8,128)(2,1)S(1)}, u32[]{:S(2)}) copy-start(bf16[336,1216]{1,0:T(8,128)(2,1)S(1)} %pad_maximum_fusion.refs_0_) | copy-start | bytes 2451460
  25.4 21.1 %collective-permute-start.7 = (bf16[96,2048]{1,0:T(8,128)(2,1)S(1)}, bf16[96,2048]{1,0:T(8,128)(2,1)}, u32[]{:S(2)}, u32[]{:S(2)}) collective-permute-start(bf16[96,2048]{1,0:T(8,128)(2,1)S(1)} %constant_dynamic-update-slice_fusion.refs_1_), channel_id=1, source_target_pairs={{0,4},{4,0},{1,5},{5,1},{2,6},{6,2},{3,7},{7,3},{8,12},{12,8},{9,1... | collective-permute-start | bytes 1179656 | tf_op jit(solution)/shard_map/ppermute | solution.py:277
  33.8 12.8 %copy-start.22 = (bf16[96,2048]{1,0:T(8,128)(2,1)}, bf16[96,2048]{1,0:T(8,128)(2,1)S(1)}, u32[]{:S(2)}) copy-start(bf16[96,2048]{1,0:T(8,128)(2,1)S(1)} %collective-permute-done.3.refs_2_) | copy-start | bytes 1179652
  33.8 12.8 %collective-permute-start.8 = (bf16[96,2048]{1,0:T(8,128)(2,1)S(1)}, bf16[96,2048]{1,0:T(8,128)(2,1)}, u32[]{:S(2)}, u32[]{:S(2)}) collective-permute-start(bf16[96,2048]{1,0:T(8,128)(2,1)S(1)} %collective-permute-done.3.refs_2_), channel_id=1, source_target_pairs={{0,4},{4,0},{1,5},{5,1},{2,6},{6,2},{3,7},{7,3},{8,12},{12,8},{9,1... | collective-permute-start | bytes 1179656 | tf_op jit(solution)/shard_map/ppermute | solution.py:277
  39.9 6.7 %copy-start.23 = (bf16[96,2048]{1,0:T(8,128)(2,1)}, bf16[96,2048]{1,0:T(8,128)(2,1)S(1)}, u32[]{:S(2)}) copy-start(bf16[96,2048]{1,0:T(8,128)(2,1)S(1)} %collective-permute-done.4.refs_3_) | copy-start | bytes 1179652
  39.9 6.7 %collective-permute-start.9 = (bf16[96,2048]{1,0:T(8,128)(2,1)S(1)}, bf16[96,2048]{1,0:T(8,128)(2,1)}, u32[]{:S(2)}, u32[]{:S(2)}) collective-permute-start(bf16[96,2048]{1,0:T(8,128)(2,1)S(1)} %collective-permute-done.4.refs_3_), channel_id=1, source_target_pairs={{0,4},{4,0},{1,5},{5,1},{2,6},{6,2},{3,7},{7,3},{8,12},{12,8},{9,1... | collective-permute-start | bytes 1179656 | tf_op jit(solution)/shard_map/ppermute | solution.py:277
  39.9 6.7 %collective-permute-start.10 = (bf16[96,2048]{1,0:T(8,128)(2,1)}, bf16[96,2048]{1,0:T(8,128)(2,1)}, u32[]{:S(2)}, u32[]{:S(2)}) collective-permute-start(bf16[96,2048]{1,0:T(8,128)(2,1)} %collective-permute-done.5.refs_4_), channel_id=1, source_target_pairs={{0,4},{4,0},{1,5},{5,1},{2,6},{6,2},{3,7},{7,3},{8,12},{12,8},{9,1... | collective-permute-start | bytes 1179656 | tf_op jit(solution)/shard_map/ppermute | solution.py:277
  40.4 42.4 %collective-permute-start.13 = (bf16[336,1216]{1,0:T(8,128)(2,1)S(1)}, bf16[336,1216]{1,0:T(8,128)(2,1)S(1)}, u32[]{:S(2)}, u32[]{:S(2)}) collective-permute-start(bf16[336,1216]{1,0:T(8,128)(2,1)S(1)} %pad_maximum_fusion.refs_0_), channel_id=1, source_target_pairs={{0,16},{8,24},{16,0},{24,8},{1,17},{9,25},{17,1},{25,9},{2,18},{10... | collective-permute-start | bytes 2451464 | tf_op jit(solution)/shard_map/ppermute | solution.py:283
  46.6 7.3 %copy-start.6 = (bf16[512,896]{1,0:T(8,128)(2,1)S(1)}, bf16[512,896]{1,0:T(8,128)(2,1)}, u32[]{:S(2)}) copy-start(bf16[512,896]{1,0:T(8,128)(2,1)} %cotangent.1) | copy-start | bytes 2752516
  53.9 30.9 %collective-permute-start.11 = (bf16[256,512]{1,0:T(8,128)(2,1)}, bf16[256,512]{1,0:T(8,128)(2,1)}, u32[]{:S(2)}, u32[]{:S(2)}) collective-permute-start(bf16[256,512]{1,0:T(8,128)(2,1)} %get-tuple-element.83.own), channel_id=1, source_target_pairs={{0,4},{4,0},{1,5},{5,1},{2,6},{6,2},{3,7},{7,3},{8,12},{12,8},{9,1... | collective-permute-start | bytes 786440 | tf_op jit(solution)/shard_map/ppermute | solution.py:277
  53.9 76.6 %collective-permute-start.22 = (bf16[512,896]{1,0:T(8,128)(2,1)S(1)}, bf16[512,896]{1,0:T(8,128)(2,1)}, u32[]{:S(2)}, u32[]{:S(2)}) collective-permute-start(bf16[512,896]{1,0:T(8,128)(2,1)S(1)} %copy-done.6), channel_id=1, source_target_pairs={{0,1},{1,0},{2,3},{3,2},{4,5},{5,4},{6,7},{7,6},{8,9},{9,8},{10,11... | collective-permute-start | bytes 2752520 | tf_op jit(solution)/shard_map/ppermute | solution.py:280
  55.0 75.7 %collective-permute-start.23 = (bf16[512,896]{1,0:T(8,128)(2,1)S(1)}, bf16[512,896]{1,0:T(8,128)(2,1)}, u32[]{:S(2)}, u32[]{:S(2)}) collective-permute-start(bf16[512,896]{1,0:T(8,128)(2,1)S(1)} %copy-done.6), channel_id=1, source_target_pairs={{0,2},{1,3},{2,0},{3,1},{4,6},{5,7},{6,4},{7,5},{8,10},{9,11},{10,... | collective-permute-start | bytes 2752520 | tf_op jit(solution)/shard_map/ppermute | solution.py:280
  82.8 18.2 %copy-start.11 = (bf16[336,1216]{1,0:T(8,128)(2,1)}, bf16[336,1216]{1,0:T(8,128)(2,1)S(1)}, u32[]{:S(2)}) copy-start(bf16[336,1216]{1,0:T(8,128)(2,1)S(1)} %collective-permute-done.13.refs_2_) | copy-start | bytes 2451460
  82.8 24.3 %collective-permute-start.14 = (bf16[336,1216]{1,0:T(8,128)(2,1)S(1)}, bf16[336,1216]{1,0:T(8,128)(2,1)S(1)}, u32[]{:S(2)}, u32[]{:S(2)}) collective-permute-start(bf16[336,1216]{1,0:T(8,128)(2,1)S(1)} %pad_maximum_fusion.refs_0_), channel_id=1, source_target_pairs={{8,16},{16,8},{9,17},{17,9},{10,18},{18,10},{11,19},{19,11},{12,20... | collective-permute-start | bytes 2451464 | tf_op jit(solution)/shard_map/ppermute | solution.py:308
  83.5 27.2 %collective-permute-start.15 = (bf16[336,1216]{1,0:T(8,128)(2,1)S(1)}, bf16[336,1216]{1,0:T(8,128)(2,1)}, u32[]{:S(2)}, u32[]{:S(2)}) collective-permute-start(bf16[336,1216]{1,0:T(8,128)(2,1)S(1)} %collective-permute-done.13.refs_2_), channel_id=1, source_target_pairs={{16,24},{8,0},{17,25},{9,1},{18,26},{10,2},{19,27},{11,3},{20,28},... | collective-permute-start | bytes 2451464 | tf_op jit(solution)/shard_map/ppermute | solution.py:309
  105.8 25.2 %collective-permute-start.20 = (bf16[512,896]{1,0:T(8,128)(2,1)}, bf16[512,896]{1,0:T(8,128)(2,1)}, u32[]{:S(2)}, u32[]{:S(2)}) collective-permute-start(bf16[512,896]{1,0:T(8,128)(2,1)} %get-tuple-element.110.refs_0_), channel_id=1, source_target_pairs={{0,1},{1,0},{2,3},{3,2},{4,5},{5,4},{6,7},{7,6},{8,9},{9,8},{10,11... | collective-permute-start | bytes 2752520 | tf_op jit(solution)/shard_map/ppermute | solution.py:280
  107.1 18.4 %collective-permute-start.12 = (bf16[336,1216]{1,0:T(8,128)(2,1)S(1)}, bf16[336,1216]{1,0:T(8,128)(2,1)}, u32[]{:S(2)}, u32[]{:S(2)}) collective-permute-start(bf16[336,1216]{1,0:T(8,128)(2,1)S(1)} %pad_maximum_fusion.refs_0_), channel_id=1, source_target_pairs={{0,8},{8,0},{16,24},{24,16},{1,9},{9,1},{17,25},{25,17},{2,10},{10... | collective-permute-start | bytes 2451464 | tf_op jit(solution)/shard_map/ppermute | solution.py:283
  110.6 20.5 %collective-permute-start.21 = (bf16[512,896]{1,0:T(8,128)(2,1)}, bf16[512,896]{1,0:T(8,128)(2,1)S(1)}, u32[]{:S(2)}, u32[]{:S(2)}) collective-permute-start(bf16[512,896]{1,0:T(8,128)(2,1)} %get-tuple-element.110.refs_0_), channel_id=1, source_target_pairs={{0,2},{1,3},{2,0},{3,1},{4,6},{5,7},{6,4},{7,5},{8,10},{9,11},{10,... | collective-permute-start | bytes 2752520 | tf_op jit(solution)/shard_map/ppermute | solution.py:280
  112.7 23.7 %copy-start.3 = (bf16[336,1216]{1,0:T(8,128)(2,1)}, bf16[336,1216]{1,0:T(8,128)(2,1)S(1)}, u32[]{:S(2)}) copy-start(bf16[336,1216]{1,0:T(8,128)(2,1)S(1)} %broadcast_select_fusion.refs_3_) | copy-start | bytes 2451460
  125.5 7.3 %collective-permute-start.16 = (bf16[336,1216]{1,0:T(8,128)(2,1)S(1)}, bf16[336,1216]{1,0:T(8,128)(2,1)S(1)}, u32[]{:S(2)}, u32[]{:S(2)}) collective-permute-start(bf16[336,1216]{1,0:T(8,128)(2,1)S(1)} %pad_maximum_fusion.refs_0_), channel_id=1, source_target_pairs={{0,4},{4,0},{1,5},{5,1},{2,6},{6,2},{3,7},{7,3},{8,12},{12,8},{9,1... | collective-permute-start | bytes 2451464 | tf_op jit(solution)/shard_map/ppermute | solution.py:277
  130.5 4.6 %collective-permute-start.18 = (bf16[336,1216]{1,0:T(8,128)(2,1)}, bf16[336,1216]{1,0:T(8,128)(2,1)}, u32[]{:S(2)}, u32[]{:S(2)}) collective-permute-start(bf16[336,1216]{1,0:T(8,128)(2,1)} %copy-done.11), channel_id=1, source_target_pairs={{0,4},{4,0},{1,5},{5,1},{2,6},{6,2},{3,7},{7,3},{8,12},{12,8},{9,1... | collective-permute-start | bytes 2451464 | tf_op jit(solution)/shard_map/ppermute | solution.py:277
  130.6 4.5 %collective-permute-start.17 = (bf16[336,1216]{1,0:T(8,128)(2,1)}, bf16[336,1216]{1,0:T(8,128)(2,1)}, u32[]{:S(2)}, u32[]{:S(2)}) collective-permute-start(bf16[336,1216]{1,0:T(8,128)(2,1)} %collective-permute-done.12.refs_1_), channel_id=1, source_target_pairs={{0,4},{4,0},{1,5},{5,1},{2,6},{6,2},{3,7},{7,3},{8,12},{12,8},{9,1... | collective-permute-start | bytes 2451464 | tf_op jit(solution)/shard_map/ppermute | solution.py:277
  131.1 5.3 %collective-permute-start.19 = (bf16[336,1216]{1,0:T(8,128)(2,1)S(1)}, bf16[336,1216]{1,0:T(8,128)(2,1)}, u32[]{:S(2)}, u32[]{:S(2)}) collective-permute-start(bf16[336,1216]{1,0:T(8,128)(2,1)S(1)} %broadcast_select_fusion.refs_3_), channel_id=1, source_target_pairs={{0,4},{4,0},{1,5},{5,1},{2,6},{6,2},{3,7},{7,3},{8,12},{12,8},{9,1... | collective-permute-start | bytes 2451464 | tf_op jit(solution)/shard_map/ppermute | solution.py:277
  131.1 54.4 %collective-permute-start.25 = (bf16[512,896]{1,0:T(8,128)(2,1)S(1)}, bf16[512,896]{1,0:T(8,128)(2,1)}, u32[]{:S(2)}, u32[]{:S(2)}) collective-permute-start(bf16[512,896]{1,0:T(8,128)(2,1)S(1)} %copy-done.6), channel_id=1, source_target_pairs={{0,3},{1,2},{2,1},{3,0},{4,7},{5,6},{6,5},{7,4},{8,11},{9,10},{10,... | collective-permute-start | bytes 2752520 | tf_op jit(solution)/shard_map/ppermute | solution.py:280
  132.8 3.6 copy-start.12
  132.8 52.7 %collective-permute-start.24 = (bf16[512,896]{1,0:T(8,128)(2,1)}, bf16[512,896]{1,0:T(8,128)(2,1)}, u32[]{:S(2)}, u32[]{:S(2)}) collective-permute-start(bf16[512,896]{1,0:T(8,128)(2,1)} %get-tuple-element.110.refs_0_), channel_id=1, source_target_pairs={{0,3},{1,2},{2,1},{3,0},{4,7},{5,6},{6,5},{7,4},{8,11},{9,10},{10,... | collective-permute-start | bytes 2752520 | tf_op jit(solution)/shard_map/ppermute | solution.py:280
  183.3 40.8 %collective-permute-start.26 = (bf16[512,896]{1,0:T(8,128)(2,1)}, bf16[512,896]{1,0:T(8,128)(2,1)S(1)}, u32[]{:S(2)}, u32[]{:S(2)}) collective-permute-start(bf16[512,896]{1,0:T(8,128)(2,1)} %get-tuple-element.116), channel_id=1, source_target_pairs={{0,1},{1,0},{2,3},{3,2},{4,5},{5,4},{6,7},{7,6},{8,9},{9,8},{10,11... | collective-permute-start | bytes 2752520 | tf_op jit(solution)/shard_map/ppermute | solution.py:280
  184.0 42.2 %collective-permute-start.27 = (bf16[512,896]{1,0:T(8,128)(2,1)}, bf16[512,896]{1,0:T(8,128)(2,1)S(1)}, u32[]{:S(2)}, u32[]{:S(2)}) collective-permute-start(bf16[512,896]{1,0:T(8,128)(2,1)} %get-tuple-element.117), channel_id=1, source_target_pairs={{0,2},{1,3},{2,0},{3,1},{4,6},{5,7},{6,4},{7,5},{8,10},{9,11},{10,... | collective-permute-start | bytes 2752520 | tf_op jit(solution)/shard_map/ppermute | solution.py:280
  200.1 26.2 %collective-permute-start.28 = (bf16[512,896]{1,0:T(8,128)(2,1)}, bf16[512,896]{1,0:T(8,128)(2,1)S(1)}, u32[]{:S(2)}, u32[]{:S(2)}) collective-permute-start(bf16[512,896]{1,0:T(8,128)(2,1)} %get-tuple-element.118), channel_id=1, source_target_pairs={{0,3},{1,2},{2,1},{3,0},{4,7},{5,6},{6,5},{7,4},{8,11},{9,10},{10,... | collective-permute-start | bytes 2752520 | tf_op jit(solution)/shard_map/ppermute | solution.py:280
  224.1 59.1 %collective-permute-start.43 = (bf16[4,3,112,1216]{3,2,1,0:T(8,128)(2,1)}, bf16[4,3,112,1216]{3,2,1,0:T(8,128)(2,1)}, u32[]{:S(2)}, u32[]{:S(2)}) collective-permute-start(bf16[4,3,112,1216]{3,2,1,0:T(8,128)(2,1)} %get-tuple-element.149), channel_id=1, source_target_pairs={{0,4},{4,0},{1,5},{5,1},{2,6},{6,2},{3,7},{7,3},{8,12},{12,8},{9,1... | collective-permute-start | bytes 9805832 | tf_op jit(solution)/shard_map/ppermute | solution.py:277
  250.2 9.3 %collective-permute-start.32 = (f32[256,512]{1,0:T(8,128)}, f32[256,512]{1,0:T(8,128)S(1)}, u32[]{:S(2)}, u32[]{:S(2)}) collective-permute-start(f32[256,512]{1,0:T(8,128)} %get-tuple-element.134), channel_id=1, source_target_pairs={{0,4},{4,0},{1,5},{5,1},{2,6},{6,2},{3,7},{7,3},{8,12},{12,8},{9,1... | collective-permute-start | bytes 1572872 | tf_op jit(solution)/shard_map/ppermute | solution.py:277
  271.5 4.4 %collective-permute-start.33 = (bf16[4,128,2048]{2,1,0:T(8,128)(2,1)}, bf16[4,128,2048]{2,1,0:T(8,128)(2,1)S(1)}, u32[]{:S(2)}, u32[]{:S(2)}) collective-permute-start(bf16[4,128,2048]{2,1,0:T(8,128)(2,1)} %get-tuple-element.141), channel_id=1, source_target_pairs={{0,4},{4,0},{1,5},{5,1},{2,6},{6,2},{3,7},{7,3},{8,12},{12,8},{9,1... | collective-permute-start | bytes 6291464 | tf_op jit(solution)/shard_map/ppermute | solution.py:277
  271.9 24.5 %collective-permute-start.31 = (bf16[512,896]{1,0:T(8,128)(2,1)}, bf16[512,896]{1,0:T(8,128)(2,1)}, u32[]{:S(2)}, u32[]{:S(2)}) collective-permute-start(bf16[512,896]{1,0:T(8,128)(2,1)} %get-tuple-element.131), channel_id=1, source_target_pairs={{0,3},{1,2},{2,1},{3,0},{4,7},{5,6},{6,5},{7,4},{8,11},{9,10},{10,... | collective-permute-start | bytes 2752520 | tf_op jit(solution)/shard_map/ppermute | solution.py:280
  273.2 42.8 %collective-permute-start.30 = (bf16[512,896]{1,0:T(8,128)(2,1)}, bf16[512,896]{1,0:T(8,128)(2,1)}, u32[]{:S(2)}, u32[]{:S(2)}) collective-permute-start(bf16[512,896]{1,0:T(8,128)(2,1)} %get-tuple-element.130), channel_id=1, source_target_pairs={{0,2},{1,3},{2,0},{3,1},{4,6},{5,7},{6,4},{7,5},{8,10},{9,11},{10,... | collective-permute-start | bytes 2752520 | tf_op jit(solution)/shard_map/ppermute | solution.py:280
  274.7 43.3 %collective-permute-start.29 = (bf16[512,896]{1,0:T(8,128)(2,1)}, bf16[512,896]{1,0:T(8,128)(2,1)}, u32[]{:S(2)}, u32[]{:S(2)}) collective-permute-start(bf16[512,896]{1,0:T(8,128)(2,1)} %get-tuple-element.129), channel_id=1, source_target_pairs={{0,1},{1,0},{2,3},{3,2},{4,5},{5,4},{6,7},{7,6},{8,9},{9,8},{10,11... | collective-permute-start | bytes 2752520 | tf_op jit(solution)/shard_map/ppermute | solution.py:280
  277.3 5.9 %copy-start.1 = (bf16[4,3,112,1216]{3,2,1,0:T(8,128)(2,1)S(1)}, bf16[4,3,112,1216]{3,2,1,0:T(8,128)(2,1)}, u32[]{:S(2)}) copy-start(bf16[4,3,112,1216]{3,2,1,0:T(8,128)(2,1)} %get-tuple-element.148) | copy-start | bytes 9805828
  281.8 45.4 %collective-permute-start.36 = (bf16[4,32,2048]{2,1,0:T(8,128)(2,1)}, bf16[4,32,2048]{2,1,0:T(8,128)(2,1)S(1)}, u32[]{:S(2)}, u32[]{:S(2)}) collective-permute-start(bf16[4,32,2048]{2,1,0:T(8,128)(2,1)} %get-tuple-element.145), channel_id=1, source_target_pairs={{0,3},{1,2},{2,1},{3,0},{4,7},{5,6},{6,5},{7,4},{8,11},{9,10},{10,... | collective-permute-start | bytes 1572872 | tf_op jit(solution)/shard_map/ppermute | solution.py:280
  283.2 13.1 %copy-start.19 = (bf16[4,32,2048]{2,1,0:T(8,128)(2,1)S(1)}, bf16[4,32,2048]{2,1,0:T(8,128)(2,1)}, u32[]{:S(2)}) copy-start(bf16[4,32,2048]{2,1,0:T(8,128)(2,1)} %get-tuple-element.143) | copy-start | bytes 1572868
  286.1 51.4 %collective-permute-start.35 = (bf16[4,32,2048]{2,1,0:T(8,128)(2,1)S(1)}, bf16[4,32,2048]{2,1,0:T(8,128)(2,1)S(1)}, u32[]{:S(2)}, u32[]{:S(2)}) collective-permute-start(bf16[4,32,2048]{2,1,0:T(8,128)(2,1)S(1)} %copy-done.20), channel_id=1, source_target_pairs={{0,2},{1,3},{2,0},{3,1},{4,6},{5,7},{6,4},{7,5},{8,10},{9,11},{10,... | collective-permute-start | bytes 1572872 | tf_op jit(solution)/shard_map/ppermute | solution.py:280
  296.3 32.5 %copy-start = (f32[512,896]{1,0:T(8,128)S(1)}, f32[512,896]{1,0:T(8,128)}, u32[]{:S(2)}) copy-start(f32[512,896]{1,0:T(8,128)} %get-tuple-element.127.hidden) | copy-start | bytes 5505028
  296.3 32.5 %copy-start.10 = (bf16[512,896]{1,0:T(8,128)(2,1)S(1)}, bf16[512,896]{1,0:T(8,128)(2,1)}, u32[]{:S(2)}) copy-start(bf16[512,896]{1,0:T(8,128)(2,1)} %get-tuple-element.128) | copy-start | bytes 2752516
  296.4 41.1 %collective-permute-start.34 = (bf16[4,32,2048]{2,1,0:T(8,128)(2,1)S(1)}, bf16[4,32,2048]{2,1,0:T(8,128)(2,1)S(1)}, u32[]{:S(2)}, u32[]{:S(2)}) collective-permute-start(bf16[4,32,2048]{2,1,0:T(8,128)(2,1)S(1)} %copy-done.19), channel_id=1, source_target_pairs={{0,1},{1,0},{2,3},{3,2},{4,5},{5,4},{6,7},{7,6},{8,9},{9,8},{10,11... | collective-permute-start | bytes 1572872 | tf_op jit(solution)/shard_map/ppermute | solution.py:280
  316.1 23.9 %collective-permute-start.46 = (bf16[3,112,1216]{2,1,0:T(8,128)(2,1)S(1)}, bf16[3,112,1216]{2,1,0:T(8,128)(2,1)S(1)}, u32[]{:S(2)}, u32[]{:S(2)}) collective-permute-start(bf16[3,112,1216]{2,1,0:T(8,128)(2,1)S(1)} %get-tuple-element.151), channel_id=1, source_target_pairs={{0,8},{8,0},{16,24},{24,16},{1,9},{9,1},{17,25},{25,17},{2,10},{10... | collective-permute-start | bytes 2451464 | tf_op jit(solution)/shard_map/ppermute | solution.py:283
  318.1 39.7 %collective-permute-start.45 = (bf16[3,112,1216]{2,1,0:T(8,128)(2,1)S(1)}, bf16[3,112,1216]{2,1,0:T(8,128)(2,1)S(1)}, u32[]{:S(2)}, u32[]{:S(2)}) collective-permute-start(bf16[3,112,1216]{2,1,0:T(8,128)(2,1)S(1)} %get-tuple-element.152), channel_id=1, source_target_pairs={{0,24},{8,16},{16,8},{24,0},{1,25},{9,17},{17,9},{25,1},{2,26},{10... | collective-permute-start | bytes 2451464 | tf_op jit(solution)/shard_map/ppermute | solution.py:283
  327.2 10.3 %copy-start.5 = (f32[4,32,2048]{2,1,0:T(8,128)S(1)}, f32[4,32,2048]{2,1,0:T(8,128)}, u32[]{:S(2)}) copy-start(f32[4,32,2048]{2,1,0:T(8,128)} %get-tuple-element.142) | copy-start | bytes 3145732
  327.2 73.3 %collective-permute-start.44 = (bf16[3,112,1216]{2,1,0:T(8,128)(2,1)S(1)}, bf16[3,112,1216]{2,1,0:T(8,128)(2,1)S(1)}, u32[]{:S(2)}, u32[]{:S(2)}) collective-permute-start(bf16[3,112,1216]{2,1,0:T(8,128)(2,1)S(1)} %get-tuple-element.150), channel_id=1, source_target_pairs={{0,16},{8,24},{16,0},{24,8},{1,17},{9,25},{17,1},{25,9},{2,18},{10... | collective-permute-start | bytes 2451464 | tf_op jit(solution)/shard_map/ppermute | solution.py:283
  337.8 63.0 %collective-permute-start.39 = (bf16[32,2048]{1,0:T(8,128)(2,1)S(1)}, bf16[32,2048]{1,0:T(8,128)(2,1)S(1)}, u32[]{:S(2)}, u32[]{:S(2)}) collective-permute-start(bf16[32,2048]{1,0:T(8,128)(2,1)S(1)} %get-tuple-element.159), channel_id=1, source_target_pairs={{0,8},{8,0},{16,24},{24,16},{1,9},{9,1},{17,25},{25,17},{2,10},{10... | collective-permute-start | bytes 393224 | tf_op jit(solution)/shard_map/ppermute | solution.py:283
  339.9 63.4 %collective-permute-start.38 = (bf16[32,2048]{1,0:T(8,128)(2,1)S(1)}, bf16[32,2048]{1,0:T(8,128)(2,1)S(1)}, u32[]{:S(2)}, u32[]{:S(2)}) collective-permute-start(bf16[32,2048]{1,0:T(8,128)(2,1)S(1)} %get-tuple-element.160), channel_id=1, source_target_pairs={{0,16},{8,24},{16,0},{24,8},{1,17},{9,25},{17,1},{25,9},{2,18},{10... | collective-permute-start | bytes 393224 | tf_op jit(solution)/shard_map/ppermute | solution.py:283
  339.9 63.4 %collective-permute-start.37 = (bf16[32,2048]{1,0:T(8,128)(2,1)S(1)}, bf16[32,2048]{1,0:T(8,128)(2,1)S(1)}, u32[]{:S(2)}, u32[]{:S(2)}) collective-permute-start(bf16[32,2048]{1,0:T(8,128)(2,1)S(1)} %get-tuple-element.158), channel_id=1, source_target_pairs={{0,24},{8,16},{16,8},{24,0},{1,25},{9,17},{17,9},{25,1},{2,26},{10... | collective-permute-start | bytes 393224 | tf_op jit(solution)/shard_map/ppermute | solution.py:283
  403.3 6.0 %collective-permute-start.40 = (bf16[32,2048]{1,0:T(8,128)(2,1)S(1)}, bf16[32,2048]{1,0:T(8,128)(2,1)S(1)}, u32[]{:S(2)}, u32[]{:S(2)}) collective-permute-start(bf16[32,2048]{1,0:T(8,128)(2,1)S(1)} %fusion.4), channel_id=1, source_target_pairs={{0,3},{1,2},{2,1},{3,0},{4,7},{5,6},{6,5},{7,4},{8,11},{9,10},{10,... | collective-permute-start | bytes 393224 | tf_op jit(solution)/shard_map/ppermute | solution.py:280
  404.8 5.9 %collective-permute-start.41 = (bf16[32,2048]{1,0:T(8,128)(2,1)S(1)}, bf16[32,2048]{1,0:T(8,128)(2,1)S(1)}, u32[]{:S(2)}, u32[]{:S(2)}) collective-permute-start(bf16[32,2048]{1,0:T(8,128)(2,1)S(1)} %fusion.4), channel_id=1, source_target_pairs={{0,2},{1,3},{2,0},{3,1},{4,6},{5,7},{6,4},{7,5},{8,10},{9,11},{10,... | collective-permute-start | bytes 393224 | tf_op jit(solution)/shard_map/ppermute | solution.py:280
  406.3 5.0 %collective-permute-start.42 = (bf16[32,2048]{1,0:T(8,128)(2,1)S(1)}, bf16[32,2048]{1,0:T(8,128)(2,1)S(1)}, u32[]{:S(2)}, u32[]{:S(2)}) collective-permute-start(bf16[32,2048]{1,0:T(8,128)(2,1)S(1)} %fusion.4), channel_id=1, source_target_pairs={{0,1},{1,0},{2,3},{3,2},{4,5},{5,4},{6,7},{7,6},{8,9},{9,8},{10,11... | collective-permute-start | bytes 393224 | tf_op jit(solution)/shard_map/ppermute | solution.py:280
  (7 other events, 11.2 us)
